TPU v7x, 512 devices: a whole 4x4x16 slice. The times are simulated.
512 devices in a mesh: seg: 16 (over y, x_hi, core), space: 32 (over z, x_lo).
Axes of the slice: x: 4 (x_hi: 2, x_lo: 2; x = x_hi * 2 + x_lo), y: 4, z: 16, core: 2. Of those that a mesh axis runs over, the one named last changes fastest.
Arguments:
- field: float32 [16, 192, 384, 128], P('seg', 'space'), may hold values from -6 to 6
- base: float32 [16, 192, 384, 128], P('seg', 'space'), may hold values from -5 to 5
- radial_step: float32 [192, 192], replicated, may hold values from -1 to 1
- az_shift: int32 [1], replicated, may hold values from 0 to 383
- ax_shift: int32 [1], replicated, may hold values from 0 to 8191
- first_segment: int32 [1], replicated, may hold values from 0 to 1023
Outputs:
- mismatch: float32 [16, 192, 384, 128], P('seg', 'space')
All inputs are finite; a program needn't handle non-finite values.
Results may differ from a plain program's by a relative error of at most 0.0001.
Values sent between devices are 32-bit elements; how exact they have to be, the bound alone decides.
No kernel may reach another device: no remote copies, remote signals or barrier semaphores. Data moves between devices by JAX's collectives and lax.ppermute only.
A program may use at most 64 MiB of HBM per device.

v0:
```python
import math

import jax
import jax.numpy as jnp
from jax import lax
from jax.sharding import PartitionSpec as P

STEPS = 2


step_size = 0.25
viscous_rate = 1.5e-05


def from_behind(block, axis, distance):
    devices = range(lax.axis_size(axis))
    route = [((i - distance) % len(devices), i) for i in devices]
    return lax.ppermute(block, axis, route)


def real_fourier(size):
    rows = jnp.arange(size, dtype=jnp.int32)
    wave = jnp.where(rows == 0, 0, jnp.where(rows == 1, size // 2, rows // 2))
    phase = wave[:, None] * rows[None, :] % size
    angle = phase.astype(jnp.float32) * jnp.float32(2.0 * math.pi / size)
    sine = (rows % 2 == 1) & (rows >= 3)
    row_scale = jnp.where(
        rows < 2, jnp.float32(math.sqrt(1.0 / size)), jnp.float32(math.sqrt(2.0 / size))
    )
    table = row_scale[:, None] * jnp.where(sine[:, None], jnp.sin(angle), jnp.cos(angle))
    return (table, wave)


def advance(state, base, radial_step, table_t, table_z, decay):
    exact = lax.Precision.HIGHEST
    for repeat in range(STEPS):
        forced = state + step_size * base * state
        spectral = jnp.einsum("mt,rtz->rmz", table_t, forced, precision=exact)
        spectral = jnp.einsum("kz,rmz->rmk", table_z, spectral, precision=exact)
        spectral = spectral * decay[None]
        mixed = jnp.einsum(
            "qr,rmk->qmk",
            radial_step,
            lax.all_to_all(spectral, "space", split_axis=1, concat_axis=0, tiled=True),
            precision=exact,
        )
        spectral = lax.all_to_all(mixed, "space", split_axis=0, concat_axis=1, tiled=True)
        state = jnp.einsum("mt,rmk->rtk", table_t, spectral, precision=exact)
        state = jnp.einsum("kz,rtk->rtz", table_z, state, precision=exact)
    return state


def reflect_shift(state, azimuth, axial):
    count_t = state.shape[1]
    count_z = state.shape[2]
    places_t = jnp.arange(count_t, dtype=jnp.int32)
    places_z = jnp.arange(count_z, dtype=jnp.int32)
    index_t = (azimuth - places_t) % count_t
    index_z = (places_z + axial) % count_z
    state = jnp.take(state, index_t, axis=1)
    return jnp.take(state, index_z, axis=2)


def shards(field, base, radial_step, az_shift, ax_shift, first_segment):
    own_state = field[0]
    own_base = base[0]
    table_t, wave_t = real_fourier(own_state.shape[1])
    table_z, wave_z = real_fourier(own_state.shape[2])
    float_t = wave_t.astype(jnp.float32)
    float_z = wave_z.astype(jnp.float32)
    decay = jnp.exp(
        jnp.float32(-viscous_rate)
        * (float_t[:, None] * float_t[:, None] + float_z[None, :] * float_z[None, :])
    )
    finished = advance(own_state, own_base, radial_step, table_t, table_z, decay)
    carried = from_behind(finished, "seg", 1)
    moved = reflect_shift(carried, az_shift[0], ax_shift[0])
    closing = lax.axis_index("seg") == first_segment[0] % lax.axis_size("seg")
    carried = jnp.where(closing, moved, carried)
    return (carried - own_state)[None]


def solution(mesh):
    in_specs = (P("seg", "space", None, None), P("seg", "space", None, None), P(), P(), P(), P())
    out_specs = P("seg", "space", None, None)
    return jax.shard_map(shards, mesh=mesh, in_specs=in_specs, out_specs=out_specs, check_vma=False)
```

profile of v0, /device:TPU:2, one launch (start us, length us, event | category | flops | bytes accessed | tf_op | source)
XLA Modules:
  0.0 419.2 jit_solution(5892955477780311300)
XLA Ops:
  0.0 0.0 copy-start
  0.1 0.1 multiply_exponential_fusion
  0.2 7.9 %convolution_bitcast_fusion.5 = f32[6,384,128]{1,2,0:T(8,128)S(1)} fusion(f32[1,6,384,128]{3,2,1,0:T(8,128)} %param.6, f32[1,6,384,128]{3,2,1,0:T(8,128)} %param.7, s32[384]{0:T(512)S(1)} %fusion.32, f32[384]{0:T(512)S(1)} %fusion.40, pred[384]{0:T(512)(128)(4,1)S(1)} %fusion.38), kind=kOutput, calls=%fused_computation.10 | convolution fusion | flops 1361461248 | bytes 3542400 | tf_op jit(solution)/shard_map/mt,rtz->rmz/dot_general | solution.py:38
  8.1 2.2 convolution_multiply_fusion.1
  10.3 0.7 copy.18
  11.1 104.3 %all_to_all.72 = f32[6,384,128]{2,0,1:T(8,128)S(1)} all-to-all(f32[6,384,128]{2,0,1:T(8,128)S(1)} %copy.18), channel_id=1, replica_groups=mesh['seg'=16,'space'=32] {'space'}, dimensions={1} | all-to-all | bytes 2359296 | tf_op jit(solution)/shard_map/all_to_all | solution.py:44
  115.4 0.1 copy.20
  115.5 0.1 all_to_all.55
  115.7 0.0 copy-done
  115.7 1.2 convolution_bitcast_fusion.4
  116.9 0.7 copy.21
  117.6 80.9 %all_to_all.73 = f32[192,12,128]{2,1,0:T(8,128)S(1)} all-to-all(f32[192,12,128]{2,1,0:T(8,128)S(1)} %copy.21), channel_id=1, replica_groups=mesh['seg'=16,'space'=32] {'space'}, dimensions={0} | all-to-all | bytes 2359296 | tf_op jit(solution)/shard_map/all_to_all | solution.py:47
  198.5 0.1 copy.23
  198.7 0.1 all_to_all.59
  198.8 0.0 copy-start.2
  198.8 4.9 %convolution_bitcast_fusion.3 = f32[6,384,128]{1,2,0:T(8,128)S(1)} fusion(f32[6,384,128]{2,1,0:T(8,128)S(1)} %all_to_all.59, s32[384]{0:T(512)S(1)} %fusion.32, f32[384]{0:T(512)S(1)} %fusion.40, pred[384]{0:T(512)(128)(4,1)S(1)} %fusion.38), kind=kOutput, calls=%fused_computation.8 | convolution fusion | flops 1360576512 | bytes 2362752 | tf_op jit(solution)/shard_map/mt,rmk->rtk/dot_general | solution.py:48
  203.7 0.0 copy-done.2
  203.7 2.2 multiply_add_fusion
  205.9 6.3 %convolution_bitcast_fusion.2 = f32[6,384,128]{1,2,0:T(8,128)S(1)} fusion(f32[6,384,128]{2,1,0:T(8,128)S(1)} %multiply_add_fusion, s32[384]{0:T(512)S(1)} %fusion.32, f32[384]{0:T(512)S(1)} %fusion.40, pred[384]{0:T(512)(128)(4,1)S(1)} %fusion.38), kind=kOutput, calls=%fused_computation.7 | convolution fusion | flops 1360576512 | bytes 2362752 | tf_op jit(solution)/shard_map/mt,rtz->rmz/dot_general | solution.py:38
  212.2 2.2 convolution_multiply_fusion
  214.5 0.7 copy.28
  215.2 81.0 %all_to_all.74 = f32[6,384,128]{2,0,1:T(8,128)S(1)} all-to-all(f32[6,384,128]{2,0,1:T(8,128)S(1)} %copy.28), channel_id=1, replica_groups=mesh['seg'=16,'space'=32] {'space'}, dimensions={1} | all-to-all | bytes 2359296 | tf_op jit(solution)/shard_map/all_to_all | solution.py:44
  296.2 0.1 copy.30
  296.3 0.1 all_to_all.63
  296.5 1.2 convolution_bitcast_fusion.1
  297.7 0.7 copy.31
  298.4 81.2 %all_to_all.75 = f32[192,12,128]{2,1,0:T(8,128)S(1)} all-to-all(f32[192,12,128]{2,1,0:T(8,128)S(1)} %copy.31), channel_id=1, replica_groups=mesh['seg'=16,'space'=32] {'space'}, dimensions={0} | all-to-all | bytes 2359296 | tf_op jit(solution)/shard_map/all_to_all | solution.py:47
  379.6 0.1 copy.33
  379.8 0.1 all_to_all.67
  379.9 4.9 %convolution_bitcast_fusion = f32[6,384,128]{1,2,0:T(8,128)S(1)} fusion(f32[6,384,128]{2,1,0:T(8,128)S(1)} %all_to_all.67, s32[384]{0:T(512)S(1)} %fusion.32, f32[384]{0:T(512)S(1)} %fusion.40, pred[384]{0:T(512)(128)(4,1)S(1)} %fusion.38), kind=kOutput, calls=%fused_computation.5 | convolution fusion | flops 1360576512 | bytes 2362752 | tf_op jit(solution)/shard_map/mt,rmk->rtk/dot_general | solution.py:48
  384.7 2.2 fusion.20
  386.9 1.9 collective-permute-start
  390.9 17.1 %collective-permute-done = f32[6,384,128]{2,1,0:T(8,128)S(1)} collective-permute-done((f32[6,384,128]{2,1,0:T(8,128)S(1)}, f32[6,384,128]{2,1,0:T(8,128)S(1)}, u32[]{:S(2)}, u32[]{:S(2)}) %collective-permute-start) | collective-permute-done | bytes 1179680 | tf_op jit(solution)/shard_map/ppermute | solution.py:18
  408.1 0.0 copy-start.3
  408.1 1.0 copy-done.3
  409.1 0.7 copy.36
  409.8 1.8 gather_fusion
  411.7 1.3 select_bitcast_fusion
  413.0 0.7 copy.37
  413.6 0.8 gather_fusion.1
  414.4 0.0 copy-start.1
  414.4 1.5 copy.38
  415.9 0.0 copy-done.1
  415.9 2.8 fusion.1
  (14 shorter events, 0.1 us)
Async XLA Ops:
  0.0 115.7 %copy-start = (f32[192,192]{1,0:T(8,128)S(1)}, f32[192,192]{1,0:T(8,128)}, u32[]{:S(2)}) copy-start(f32[192,192]{1,0:T(8,128)} %param.8) | copy-start | bytes 442372
  198.8 4.9 %copy-start.2 = (f32[1,6,384,128]{3,2,1,0:T(8,128)S(1)}, f32[1,6,384,128]{3,2,1,0:T(8,128)}, u32[]{:S(2)}) copy-start(f32[1,6,384,128]{3,2,1,0:T(8,128)} %param.7) | copy-start | bytes 3538948
  386.9 21.1 %collective-permute-start = (f32[6,384,128]{2,1,0:T(8,128)S(1)}, f32[6,384,128]{2,1,0:T(8,128)S(1)}, u32[]{:S(2)}, u32[]{:S(2)}) collective-permute-start(f32[6,384,128]{2,1,0:T(8,128)S(1)} %fusion.20), channel_id=1, source_target_pairs={{480,0},{0,32},{32,64},{64,96},{96,128},{128,160},{160,192},{192,2... | collective-permute-start | bytes 3538952 | tf_op jit(solution)/shard_map/ppermute | solution.py:18
  408.1 1.0 copy-start.3
  414.4 1.5 copy-start.1
where the time goes:
time: 427 us; the launch traced here: 419 us
  blocking collectives  347 us (81%)
  matrix products  35.2 us (8%)
  waiting for transfers between devices  17.1 us (4%)
  local copies, waits for them, and re-layouts  10.4 us (2%)
  other arithmetic  4.35 us (1%)
    all_to_all x2, blocking collectives, advance(): lax.all_to_all(spectral, 'space', split_axis=1, concat_axis=0, tiled=True)  185 us
    all_to_all x2, blocking collectives, advance(): lax.all_to_all(mixed, 'space', split_axis=0, concat_axis=1, tiled=True)  162 us
    ppermute x1, waiting for transfers between devices, from_behind(): return lax.ppermute(block, axis, route)  17.1 us
    dot_general x2, matrix products, advance(): spectral = jnp.einsum('mt,rtz->rmz', table_t, forced, precision=exact)  14.2 us
    dot_general x2, matrix products, advance(): state = jnp.einsum('mt,rmk->rtk', table_t, spectral, precision=exact)  9.72 us
  transfers between devices with their start and end apart: 1, of which 1 were waited for; matrix products, arithmetic and copies ran while one was open for 0% of the time, Pallas kernels for 0%

commit v1 on v0

v1 whole, which is shorter than its diff:
```python
import math

import jax
import jax.numpy as jnp
import numpy as np
from jax import lax
from jax.sharding import PartitionSpec as P

STEP_SIZE = 0.25
VISCOUS_RATE = 1.5e-05
EXACT = lax.Precision.HIGHEST


def filter_table(size):
    rows = np.arange(size)
    wave = np.where(rows == 0, 0, np.where(rows == 1, size // 2, rows // 2))
    angle = (wave[:, None] * rows[None, :] % size) * (2.0 * math.pi / size)
    sine = (rows % 2 == 1) & (rows >= 3)
    scale = np.where(rows < 2, math.sqrt(1.0 / size), math.sqrt(2.0 / size))
    table = scale[:, None] * np.where(sine[:, None], np.sin(angle), np.cos(angle))
    decay = np.exp(-VISCOUS_RATE * wave.astype(np.float64) ** 2)
    return (table.T @ (decay[:, None] * table)).astype(np.float32)


def from_behind(block, axis, distance):
    devices = range(lax.axis_size(axis))
    route = [((i - distance) % len(devices), i) for i in devices]
    return lax.ppermute(block, axis, route)


def to_points(block, parts):
    radii, count_t, count_z = block.shape
    share = count_t // parts
    packed = block.reshape(radii, parts, share, count_z).swapaxes(0, 1)
    packed = packed.reshape(parts, radii * share, count_z)
    packed = lax.all_to_all(packed, "space", 0, 0, tiled=True)
    return packed.reshape(parts * radii, share, count_z)


def to_radii(block, parts):
    count_r, share, count_z = block.shape
    radii = count_r // parts
    packed = block.reshape(parts, radii * share, count_z)
    packed = lax.all_to_all(packed, "space", 0, 0, tiled=True)
    packed = packed.reshape(parts, radii, share, count_z).swapaxes(0, 1)
    return packed.reshape(radii, parts * share, count_z)


def apply_filter(state, table_t, table_z):
    state = jnp.einsum("ts,rsz->rtz", table_t, state, precision=EXACT)
    return jnp.einsum("rtz,zk->rtk", state, table_z, precision=EXACT)


def shards(field, base, radial_step, az_shift, ax_shift, first_segment):
    state = field[0]
    own_base = base[0]
    count_t, count_z = state.shape[1:]
    parts = lax.axis_size("space")
    table_t = jnp.asarray(filter_table(count_t))
    table_z = jnp.asarray(filter_table(count_z))

    with jax.named_scope("first_filter"):
        filtered = apply_filter(state + STEP_SIZE * own_base * state, table_t, table_z)
    with jax.named_scope("shift_state"):
        filtered = from_behind(filtered, "seg", 1)
    with jax.named_scope("base_to_points"):
        base_points = to_points(own_base, parts)
    with jax.named_scope("shift_base"):
        base_points = from_behind(base_points, "seg", 1)
    with jax.named_scope("state_to_points"):
        points = to_points(filtered, parts)
    with jax.named_scope("radial"):
        points = jnp.einsum("qr,rtz->qtz", radial_step, points, precision=EXACT)
        points = points + STEP_SIZE * base_points * points
        points = jnp.einsum("qr,rtz->qtz", radial_step, points, precision=EXACT)
    with jax.named_scope("state_to_radii"):
        carried = to_radii(points, parts)

    with jax.named_scope("closing_tables"):
        closing = lax.axis_index("seg") == first_segment[0] % lax.axis_size("seg")
        places_t = jnp.arange(count_t, dtype=jnp.int32)
        places_z = jnp.arange(count_z, dtype=jnp.int32)
        index_t = jnp.where(closing, (az_shift[0] - places_t) % count_t, places_t)
        index_z = jnp.where(closing, (places_z + ax_shift[0]) % count_z, places_z)
        last_t = jnp.take(table_t, index_t, axis=0)
        last_z = jnp.take(table_z, index_z, axis=0).T
    with jax.named_scope("last_filter"):
        carried = apply_filter(carried, last_t, last_z)
    return (carried - state)[None]


def solution(mesh):
    in_specs = (P("seg", "space", None, None), P("seg", "space", None, None), P(), P(), P(), P())
    out_specs = P("seg", "space", None, None)
    return jax.shard_map(shards, mesh=mesh, in_specs=in_specs, out_specs=out_specs, check_vma=False)
```

time: 427 us -> 224 us (0.52)
  the two profiles are of different devices: /device:TPU:2 before, /device:TPU:1 now
where the time goes in v1:
time: 224 us; the launch traced here: 222 us
  waiting for transfers between devices  148 us (66%)
  starting transfers between devices  39.6 us (18%)
  matrix products  17 us (8%)
  local copies, waits for them, and re-layouts  15.5 us (7%)
  between operations  2.24 us (1%)
    all_to_all x2, waiting for transfers between devices, to_points(): packed = lax.all_to_all(packed, 'space', 0, 0, tiled=True)  78.2 us
    all_to_all x1, waiting for transfers between devices, to_radii(): packed = lax.all_to_all(packed, 'space', 0, 0, tiled=True)  53.5 us
    all_to_all x2, starting transfers between devices, to_points(): packed = lax.all_to_all(packed, 'space', 0, 0, tiled=True)  23 us
    ppermute x2, waiting for transfers between devices, from_behind(): return lax.ppermute(block, axis, route)  15.8 us
    ppermute x2, starting transfers between devices, from_behind(): return lax.ppermute(block, axis, route)  10.8 us
    dot_general x2, matrix products, apply_filter(): state = jnp.einsum('ts,rsz->rtz', table_t, state, precision=EXACT)  9.08 us
    all_to_all x1, starting transfers between devices, to_radii(): packed = lax.all_to_all(packed, 'space', 0, 0, tiled=True)  5.83 us
    dot_general x2, matrix products, apply_filter(): return jnp.einsum('rtz,zk->rtk', state, table_z, precision=EXACT)  5.07 us
  transfers between devices with their start and end apart: 5, of which 4 were waited for; matrix products, arithmetic and copies ran while one was open for 8% of the time, Pallas kernels for 0%

profile of v1, /device:TPU:1, one launch (start us, length us, event | category | flops | bytes accessed | tf_op | source)
XLA Modules:
  0.0 222.0 jit_solution(1327085884287145989)
XLA Ops:
  0.0 0.0 copy-start
  0.0 1.4 reshape_squeeze.3
  1.4 0.4 copy.23
  1.8 1.7 copy.24
  3.5 0.0 copy-start.2
  3.5 0.0 copy-start.5
  3.5 17.1 %all-to-all-start.1 = ((f32[32,72,128]{2,1,0:T(8,128)}), f32[32,72,128]{2,1,0:T(8,128)S(1)}, u32[]{:S(2)}, u32[]{:S(2)}) async-start(f32[32,72,128]{2,1,0:T(8,128)} %copy.24), calls=%async_computation.1 | async-start | bytes 2359296 | tf_op jit(solution)/shard_map/base_to_points/all_to_all | solution.py:36
  20.6 0.0 copy-done.2
  20.6 0.0 copy-done.5
  20.6 0.0 copy-start.7
  20.6 5.2 %convolution_bitcast_fusion.3 = f32[6,384,128]{1,2,0:T(8,128)S(1)} fusion(f32[384,384,1]{1,0,2:T(8,128)S(1)} %copy-done.5, f32[1,6,384,128]{3,2,1,0:T(8,128)} %param.8, f32[1,6,384,128]{3,2,1,0:T(8,128)S(1)} %copy-done.2), kind=kOutput, calls=%fused_computation.7 | convolution fusion | flops 1359839232 | bytes 4128768 | tf_op jit(solution)/shard_map/first_filter/ts,rsz->rtz/dot_general | solution.py:50
  25.8 0.0 copy-done.7
  25.8 2.0 fusion.30
  27.8 5.2 %collective-permute-start = (f32[6,384,128]{2,1,0:T(8,128)S(1)}, f32[6,384,128]{2,1,0:T(8,128)}, u32[]{:S(2)}, u32[]{:S(2)}) collective-permute-start(f32[6,384,128]{2,1,0:T(8,128)S(1)} %fusion.30), channel_id=1, source_target_pairs={{480,0},{0,32},{32,64},{64,96},{96,128},{128,160},{160,192},{192,2... | collective-permute-start | bytes 3538952 | tf_op jit(solution)/shard_map/shift_state/ppermute | solution.py:28
  33.0 15.8 %collective-permute-done = f32[6,384,128]{2,1,0:T(8,128)} collective-permute-done((f32[6,384,128]{2,1,0:T(8,128)S(1)}, f32[6,384,128]{2,1,0:T(8,128)}, u32[]{:S(2)}, u32[]{:S(2)}) %collective-permute-start) | collective-permute-done | bytes 1179680 | tf_op jit(solution)/shard_map/shift_state/ppermute | solution.py:28
  48.8 1.3 reshape.131
  50.2 0.4 copy.20
  50.5 1.7 copy.21
  52.2 26.8 %all-to-all-done.1 = f32[32,72,128]{2,1,0:T(8,128)S(1)} async-done(((f32[32,72,128]{2,1,0:T(8,128)}), f32[32,72,128]{2,1,0:T(8,128)S(1)}, u32[]{:S(2)}, u32[]{:S(2)}) %all-to-all-start.1) | async-done | bytes 1179680 | tf_op jit(solution)/shard_map/base_to_points/all_to_all | solution.py:36
  79.0 5.9 %all-to-all-start = ((f32[32,72,128]{2,1,0:T(8,128)}), f32[32,72,128]{2,1,0:T(8,128)}, u32[]{:S(2)}, u32[]{:S(2)}) async-start(f32[32,72,128]{2,1,0:T(8,128)} %copy.21), calls=%async_computation | async-start | bytes 2359296 | tf_op jit(solution)/shard_map/state_to_points/all_to_all | solution.py:36
  84.9 0.1 reshape.135
  85.0 1.4 copy.25
  86.4 5.6 %collective-permute-start.1 = (f32[192,12,128]{2,0,1:T(8,128)}, f32[192,12,128]{2,0,1:T(8,128)S(1)}, u32[]{:S(2)}, u32[]{:S(2)}) collective-permute-start(f32[192,12,128]{2,0,1:T(8,128)} %copy.25), channel_id=1, source_target_pairs={{480,0},{0,32},{32,64},{64,96},{96,128},{128,160},{160,192},{192,2... | collective-permute-start | bytes 3538952 | tf_op jit(solution)/shard_map/shift_base/ppermute | solution.py:28
  92.0 51.4 %all-to-all-done = f32[32,72,128]{2,1,0:T(8,128)} async-done(((f32[32,72,128]{2,1,0:T(8,128)}), f32[32,72,128]{2,1,0:T(8,128)}, u32[]{:S(2)}, u32[]{:S(2)}) %all-to-all-start) | async-done | bytes 1179680 | tf_op jit(solution)/shard_map/state_to_points/all_to_all | solution.py:36
  143.5 1.3 reshape.133
  144.8 0.0 copy-done
  144.8 1.5 convolution_bitcast_fusion.2
  146.3 0.0 collective-permute-done.1
  146.3 1.3 convolution_bitcast_fusion.1
  147.7 0.7 copy.26
  148.4 1.1 reshape.136
  149.5 0.0 copy-start.1
  149.5 5.8 %all-to-all-start.2 = ((f32[32,72,128]{2,1,0:T(8,128)}), f32[32,72,128]{2,1,0:T(8,128)S(1)}, u32[]{:S(2)}, u32[]{:S(2)}) async-start(f32[32,72,128]{2,1,0:T(8,128)} %reshape.136), calls=%async_computation.2 | async-start | bytes 2359296 | tf_op jit(solution)/shard_map/state_to_radii/all_to_all | solution.py:44
  157.3 0.0 copy-done.1
  157.3 0.0 copy-start.4
  157.4 1.7 gather_fusion
  159.1 0.0 copy-done.4
  159.1 1.2 gather_fusion.1
  160.4 53.5 %all-to-all-done.2 = f32[32,72,128]{2,1,0:T(8,128)S(1)} async-done(((f32[32,72,128]{2,1,0:T(8,128)}), f32[32,72,128]{2,1,0:T(8,128)S(1)}, u32[]{:S(2)}, u32[]{:S(2)}) %all-to-all-start.2) | async-done | bytes 1179680 | tf_op jit(solution)/shard_map/state_to_radii/all_to_all | solution.py:44
  213.9 0.2 copy.27
  214.1 0.7 copy.28
  214.8 0.1 reshape.138
  214.9 0.0 copy-start.3
  214.9 0.0 copy-start.6
  215.0 3.9 %convolution_bitcast_fusion = f32[6,384,128]{1,2,0:T(8,128)S(1)} fusion(f32[6,384,128]{2,1,0:T(8,128)S(1)} %reshape.138, f32[384,384]{1,0:T(8,128)S(1)} %gather_fusion, pred[384]{0:T(512)(128)(4,1)S(1)} %compare_and_fusion.1), kind=kOutput, calls=%fused_computation.4 | convolution fusion | flops 1359101952 | bytes 2949504 | tf_op jit(solution)/shard_map/last_filter/ts,rsz->rtz/dot_general | solution.py:50
  218.9 0.0 copy-done.3
  218.9 0.0 copy-done.6
  218.9 3.1 %fusion = f32[1,6,384,128]{3,2,1,0:T(8,128)} fusion(f32[6,384,128]{1,2,0:T(8,128)S(1)} %convolution_bitcast_fusion, f32[1,6,384,128]{3,2,1,0:T(8,128)S(1)} %copy-done.3, f32[128,128]{1,0:T(8,128)S(1)} %copy-done.6, pred[128]{0:T(512)(128)(4,1)S(1)} %compare_and_fusion), kind=kOutput, calls=%fused_computation.9 | convolution fusion | flops 453296128 | bytes 3604608 | tf_op jit(solution)/shard_map/last_filter/rtz,zk->rtk/dot_general | solution.py:51
  (6 shorter events, 0.1 us)
Async XLA Ops:
  0.0 144.8 %copy-start = (f32[192,192]{1,0:T(8,128)S(1)}, f32[192,192]{1,0:T(8,128)}, u32[]{:S(2)}) copy-start(f32[192,192]{1,0:T(8,128)} %param.10) | copy-start | bytes 442372
  3.5 17.1 %copy-start.2 = (f32[1,6,384,128]{3,2,1,0:T(8,128)S(1)}, f32[1,6,384,128]{3,2,1,0:T(8,128)}, u32[]{:S(2)}) copy-start(f32[1,6,384,128]{3,2,1,0:T(8,128)} %param.9) | copy-start | bytes 3538948
  3.5 17.1 %copy-start.5 = (f32[384,384,1]{1,0,2:T(8,128)S(1)}, f32[384,384,1]{1,0,2:T(8,128)}, u32[]{:S(2)}) copy-start(f32[384,384,1]{1,0,2:T(8,128)} %constant.83) | copy-start | bytes 1769476
  3.5 75.6 %all-to-all-start.1 = ((f32[32,72,128]{2,1,0:T(8,128)}), f32[32,72,128]{2,1,0:T(8,128)S(1)}, u32[]{:S(2)}, u32[]{:S(2)}) async-start(f32[32,72,128]{2,1,0:T(8,128)} %copy.24), calls=%async_computation.1 | async-start | bytes 2359296 | tf_op jit(solution)/shard_map/base_to_points/all_to_all | solution.py:36
  20.6 5.2 %copy-start.7 = (f32[128,128,1]{1,0,2:T(8,128)S(1)}, f32[128,128,1]{1,0,2:T(8,128)}, u32[]{:S(2)}) copy-start(f32[128,128,1]{1,0,2:T(8,128)} %constant.84) | copy-start | bytes 196612
  27.8 21.0 %collective-permute-start = (f32[6,384,128]{2,1,0:T(8,128)S(1)}, f32[6,384,128]{2,1,0:T(8,128)}, u32[]{:S(2)}, u32[]{:S(2)}) collective-permute-start(f32[6,384,128]{2,1,0:T(8,128)S(1)} %fusion.30), channel_id=1, source_target_pairs={{480,0},{0,32},{32,64},{64,96},{96,128},{128,160},{160,192},{192,2... | collective-permute-start | bytes 3538952 | tf_op jit(solution)/shard_map/shift_state/ppermute | solution.py:28
  79.0 64.4 %all-to-all-start = ((f32[32,72,128]{2,1,0:T(8,128)}), f32[32,72,128]{2,1,0:T(8,128)}, u32[]{:S(2)}, u32[]{:S(2)}) async-start(f32[32,72,128]{2,1,0:T(8,128)} %copy.21), calls=%async_computation | async-start | bytes 2359296 | tf_op jit(solution)/shard_map/state_to_points/all_to_all | solution.py:36
  86.4 59.9 %collective-permute-start.1 = (f32[192,12,128]{2,0,1:T(8,128)}, f32[192,12,128]{2,0,1:T(8,128)S(1)}, u32[]{:S(2)}, u32[]{:S(2)}) collective-permute-start(f32[192,12,128]{2,0,1:T(8,128)} %copy.25), channel_id=1, source_target_pairs={{480,0},{0,32},{32,64},{64,96},{96,128},{128,160},{160,192},{192,2... | collective-permute-start | bytes 3538952 | tf_op jit(solution)/shard_map/shift_base/ppermute | solution.py:28
  149.5 7.9 %copy-start.1 = (f32[384,384]{1,0:T(8,128)S(1)}, f32[384,384]{1,0:T(8,128)}, u32[]{:S(2)}) copy-start(f32[384,384]{1,0:T(8,128)} %constant.79.clone) | copy-start | bytes 1769476
  149.5 64.4 %all-to-all-start.2 = ((f32[32,72,128]{2,1,0:T(8,128)}), f32[32,72,128]{2,1,0:T(8,128)S(1)}, u32[]{:S(2)}, u32[]{:S(2)}) async-start(f32[32,72,128]{2,1,0:T(8,128)} %reshape.136), calls=%async_computation.2 | async-start | bytes 2359296 | tf_op jit(solution)/shard_map/state_to_radii/all_to_all | solution.py:44
  157.3 1.8 copy-start.4
  214.9 4.0 %copy-start.3 = (f32[1,6,384,128]{3,2,1,0:T(8,128)S(1)}, f32[1,6,384,128]{3,2,1,0:T(8,128)}, u32[]{:S(2)}) copy-start(f32[1,6,384,128]{3,2,1,0:T(8,128)} %param.8) | copy-start | bytes 3538948
  214.9 4.0 %copy-start.6 = (f32[128,128]{1,0:T(8,128)S(1)}, f32[128,128]{1,0:T(8,128)}, u32[]{:S(2)}) copy-start(f32[128,128]{1,0:T(8,128)} %gather_fusion.1) | copy-start | bytes 196612

commit v2 on v1

v2 whole, which is shorter than its diff:
```python
import math

import jax
import jax.numpy as jnp
import ml_dtypes
import numpy as np
from jax import lax
from jax.experimental import pallas as pl
from jax.experimental.pallas import tpu as pltpu
from jax.sharding import PartitionSpec as P

STEP_SIZE = 0.25
VISCOUS_RATE = 1.5e-05
STAGGER = 0
TILE = 8


def filter_table(size):
    rows = np.arange(size)
    wave = np.where(rows == 0, 0, np.where(rows == 1, size // 2, rows // 2))
    angle = (wave[:, None] * rows[None, :] % size) * (2.0 * math.pi / size)
    sine = (rows % 2 == 1) & (rows >= 3)
    scale = np.where(rows < 2, math.sqrt(1.0 / size), math.sqrt(2.0 / size))
    table = scale[:, None] * np.where(sine[:, None], np.sin(angle), np.cos(angle))
    decay = np.exp(-VISCOUS_RATE * wave.astype(np.float64) ** 2)
    return (table.T @ (decay[:, None] * table)).astype(np.float32)


def split_constant(table):
    high = table.astype(ml_dtypes.bfloat16)
    return high, (table - high.astype(np.float32)).astype(ml_dtypes.bfloat16)


def split_array(array):
    high = lax.reduce_precision(array, 8, 7)
    return high.astype(jnp.bfloat16), (array - high).astype(jnp.bfloat16)


def split(value):
    high = value.astype(jnp.bfloat16)
    return high, (value - high.astype(jnp.float32)).astype(jnp.bfloat16)


def product(left, right):
    (left_high, left_low), (right_high, right_low) = left, right

    def dot(a, b):
        return jnp.dot(a, b, preferred_element_type=jnp.float32)

    return dot(left_high, right_high) + (dot(left_high, right_low) + dot(left_low, right_high))


def from_behind(block, axis, distance):
    devices = range(lax.axis_size(axis))
    route = [((i - distance) % len(devices), i) for i in devices]
    return lax.ppermute(block, axis, route)


def pack_pair(out_ref, first, second):
    parts = out_ref.shape[0]
    whole = parts * TILE
    count_z = first.shape[1]
    out_ref[:, 0:8, :] = first[:whole].reshape(parts, TILE, count_z)
    out_ref[:, 8:16, :] = second[:whole].reshape(parts, TILE, count_z)
    first = first[whole:].reshape(parts // 2, TILE, count_z)
    second = second[whole:].reshape(parts // 2, TILE, count_z)
    lower = lax.broadcasted_iota(jnp.int32, first.shape, 1) < TILE // 2
    even = jnp.where(lower, first, pltpu.roll(second, TILE // 2, 1))
    odd = jnp.where(lower, pltpu.roll(first, TILE // 2, 1), second)
    for k in range(parts // 2):
        out_ref[2 * k, 16:24, :] = even[k]
        out_ref[2 * k + 1, 16:24, :] = odd[k]


def unpack_pair(ref):
    parts, _, count_z = ref.shape
    whole = parts * TILE
    first = ref[:, 0:8, :].reshape(whole, count_z)
    second = ref[:, 8:16, :].reshape(whole, count_z)
    even = jnp.stack([ref[2 * k, 16:24, :] for k in range(parts // 2)])
    odd = jnp.stack([ref[2 * k + 1, 16:24, :] for k in range(parts // 2)])
    lower = lax.broadcasted_iota(jnp.int32, even.shape, 1) < TILE // 2
    first_rest = jnp.where(lower, even, pltpu.roll(odd, TILE // 2, 1)).reshape(whole // 2, count_z)
    second_rest = jnp.where(lower, pltpu.roll(even, TILE // 2, 1), odd).reshape(whole // 2, count_z)
    return jnp.concatenate([first, first_rest], 0), jnp.concatenate([second, second_rest], 0)


def filter_pair(first, second, table_t, table_z):
    count_z = first.shape[1]
    first = product(split(first), table_z)
    second = product(split(second), table_z)
    both = product(table_t, split(jnp.concatenate([first, second], 1)))
    return both[:, :count_z], both[:, count_z:]


def first_body(late_ref, field_ref, base_ref, th_ref, tl_ref, zh_ref, zl_ref, state_ref, base_out_ref):
    pack_pair(base_out_ref, base_ref[0], base_ref[1])
    forced = [field_ref[k] + STEP_SIZE * base_ref[k] * field_ref[k] for k in range(2)]
    table_t = (th_ref[...], tl_ref[...])
    table_z = (zh_ref[...], zl_ref[...])
    pack_pair(state_ref, *filter_pair(*forced, table_t, table_z))

    @pl.when(pl.program_id(0) == pl.num_programs(0) - 1)
    def _():
        pl.delay(late_ref[0])


def first_stage(field, base, table_t, table_z, parts, late):
    radii, count_t, count_z = field.shape
    plane = pl.BlockSpec((2, count_t, count_z), lambda p: (p, 0, 0))
    packed = pl.BlockSpec((parts, 24, count_z), lambda p: (0, p, 0))
    whole_t = pl.BlockSpec((count_t, count_t), lambda p: (0, 0))
    whole_z = pl.BlockSpec((count_z, count_z), lambda p: (0, 0))
    shape = jax.ShapeDtypeStruct((parts, 12 * radii, count_z), jnp.float32)
    return pl.pallas_call(
        first_body,
        out_shape=(shape, shape),
        grid=(radii // 2,),
        in_specs=[pl.BlockSpec(memory_space=pltpu.SMEM), plane, plane, whole_t, whole_t, whole_z, whole_z],
        out_specs=(packed, packed),
        name="first_stage",
    )(late, field, base, *table_t, *table_z)


def row_of(pair, half, point):
    return 24 * pair + (TILE * half + point if point < TILE else 2 * TILE + 4 * half + point - TILE)


def load_points(ref, point, parts):
    stride = ref.shape[0] // parts
    rows = [ref[pl.ds(row_of(p, e, point), parts, stride), :] for p in range(3) for e in range(2)]
    return jnp.concatenate(rows, 0)


def coefficient_body(base_ref, out_ref):
    parts = out_ref.shape[1] // 6
    for point in range(out_ref.shape[0]):
        out_ref[point] = 1.0 + STEP_SIZE * load_points(base_ref, point, parts)


def coefficient_stage(base, parts):
    rows, count_z = base.shape
    vmem = pl.BlockSpec(memory_space=pltpu.VMEM)
    return pl.pallas_call(
        coefficient_body,
        out_shape=jax.ShapeDtypeStruct((12, rows // 12, count_z), jnp.float32),
        in_specs=[vmem],
        out_specs=vmem,
        name="coefficient_stage",
    )(base)


def radial_body(state_ref, scale_ref, high_ref, low_ref, out_ref):
    parts = scale_ref.shape[1] // 6
    count_z = scale_ref.shape[2]
    stride = out_ref.shape[0] // parts
    mix = (high_ref[...], low_ref[...])
    for point in range(0, scale_ref.shape[0], 2):
        state = jnp.concatenate([load_points(state_ref, point + k, parts) for k in range(2)], 1)
        scale = jnp.concatenate([scale_ref[point + k] for k in range(2)], 1)
        state = product(mix, split(state)) * scale
        state = product(mix, split(state))
        for k in range(2):
            for p in range(3):
                for e in range(2):
                    radius = (2 * p + e) * parts
                    out_ref[pl.ds(row_of(p, e, point + k), parts, stride), :] = state[
                        radius : radius + parts, k * count_z : (k + 1) * count_z
                    ]


def radial_stage(state, scale, mix):
    vmem = pl.BlockSpec(memory_space=pltpu.VMEM)
    return pl.pallas_call(
        radial_body,
        out_shape=jax.ShapeDtypeStruct(state.shape, jnp.float32),
        in_specs=[vmem] * 4,
        out_specs=vmem,
        name="radial_stage",
    )(state, scale, *mix)


def last_body(state_ref, field_ref, th_ref, tl_ref, zh_ref, zl_ref, out_ref):
    table_t = (th_ref[...], tl_ref[...])
    table_z = (zh_ref[...], zl_ref[...])
    first, second = filter_pair(*unpack_pair(state_ref), table_t, table_z)
    out_ref[0] = first - field_ref[0]
    out_ref[1] = second - field_ref[1]


def last_stage(state, field, table_t, table_z, parts):
    radii, count_t, count_z = field.shape
    plane = pl.BlockSpec((2, count_t, count_z), lambda p: (p, 0, 0))
    packed = pl.BlockSpec((parts, 24, count_z), lambda p: (0, p, 0))
    whole_t = pl.BlockSpec((count_t, count_t), lambda p: (0, 0))
    whole_z = pl.BlockSpec((count_z, count_z), lambda p: (0, 0))
    return pl.pallas_call(
        last_body,
        out_shape=jax.ShapeDtypeStruct(field.shape, jnp.float32),
        grid=(radii // 2,),
        in_specs=[packed, plane, whole_t, whole_t, whole_z, whole_z],
        out_specs=plane,
        name="last_stage",
    )(state, field, *table_t, *table_z)


def swap(packed):
    return lax.all_to_all(packed, "space", 0, 0, tiled=True)


def shards(field, base, radial_step, az_shift, ax_shift, first_segment):
    state = field[0]
    count_t, count_z = state.shape[1:]
    parts = lax.axis_size("space")
    segment = lax.axis_index("seg")
    table_t = filter_table(count_t)
    table_z = filter_table(count_z)

    late = (STAGGER * (segment % 2)).astype(jnp.int32)[None]
    with jax.named_scope("first_filter"):
        filtered, base_packed = first_stage(
            state, base[0], split_constant(table_t), split_constant(table_z), parts, late
        )
    with jax.named_scope("shift_state"):
        filtered = from_behind(filtered, "seg", 1)
    with jax.named_scope("base_to_points"):
        base_points = swap(base_packed)
    with jax.named_scope("shift_base"):
        scale = coefficient_stage(base_points.reshape(-1, count_z), parts)
        scale = from_behind(scale, "seg", 1)
    with jax.named_scope("state_to_points"):
        points = swap(filtered)
    with jax.named_scope("radial"):
        mix = radial_step.reshape(parts, 6, parts, 6).transpose(1, 0, 3, 2).reshape(radial_step.shape)
        points = radial_stage(points.reshape(-1, count_z), scale, split_array(mix))
    with jax.named_scope("state_to_radii"):
        carried = swap(points.reshape(parts, -1, count_z))

    with jax.named_scope("closing_tables"):
        closing = segment == first_segment[0] % lax.axis_size("seg")
        places_t = jnp.arange(count_t, dtype=jnp.int32)
        places_z = jnp.arange(count_z, dtype=jnp.int32)
        index_t = jnp.where(closing, (az_shift[0] - places_t) % count_t, places_t)
        index_z = jnp.where(closing, (places_z + ax_shift[0]) % count_z, places_z)
        last_t = split_array(jnp.take(jnp.asarray(table_t), index_t, axis=0))
        last_z = split_array(jnp.take(jnp.asarray(table_z), index_z, axis=0).T)
    with jax.named_scope("last_filter"):
        return last_stage(carried, state, last_t, last_z, parts)[None]


def solution(mesh):
    in_specs = (P("seg", "space", None, None), P("seg", "space", None, None), P(), P(), P(), P())
    out_specs = P("seg", "space", None, None)
    return jax.shard_map(shards, mesh=mesh, in_specs=in_specs, out_specs=out_specs, check_vma=False)
```

time: 224 us -> 222 us (level)
  matrix products: 17 us -> 0 us
  Pallas kernels: 0 us -> 16.6 us
  local copies, waits for them, and re-layouts: 15.5 us -> 10.4 us
  other arithmetic: 0.1 us -> 2.46 us
    dot_general x6 -> x0, matrix products: 17 us -> none  [the longest x2 9.08 us: apply_filter(): state = jnp.einsum('ts,rsz->rtz', table_t, state, precision=EXACT)]
    pallas_call x0 -> x4, Pallas kernels: none -> 16.6 us  [the longest x1 5.2 us: first_stage(): pl.pallas_call(first_body, out_shape=(shape, shape), grid=(radii // 2,),...]
    reshape x8 -> x2, local copies, waits for them, and re-layouts: 8.76 us -> 4.66 us  [shards(): radial_step.reshape(parts, 6, parts, 6).transpose(1, 0, 3, 2)]
    convert_element_type x0 -> x3, other arithmetic: none -> 2.36 us  [split_array(): return (high.astype(jnp.bfloat16), (array - high).astype(jnp.bfloat16))]
  transfers between devices with their start and end apart: 5 -> 5, of which waited for: 4 -> 4; matrix products, arithmetic and copies ran while one was open for 8% -> 5% of each run, Pallas kernels for 0% -> 1%
where the time goes in v2:
time: 222 us; the launch traced here: 219 us
  waiting for transfers between devices  148 us (67%)
  starting transfers between devices  39.4 us (18%)
  Pallas kernels  16.6 us (7%)
  local copies, waits for them, and re-layouts  10.4 us (5%)
  other arithmetic  2.46 us (1%)
    all_to_all x3, waiting for transfers between devices, swap(): return lax.all_to_all(packed, 'space', 0, 0, tiled=True)  132 us
    all_to_all x3, starting transfers between devices, swap(): return lax.all_to_all(packed, 'space', 0, 0, tiled=True)  28.8 us
    ppermute x2, waiting for transfers between devices, from_behind(): return lax.ppermute(block, axis, route)  16.7 us
    ppermute x2, starting transfers between devices, from_behind(): return lax.ppermute(block, axis, route)  10.6 us
    pallas_call x1, Pallas kernels, first_stage(): pl.pallas_call(first_body, out_shape=(shape, shape), grid=(radii // 2,),...  5.2 us
    pallas_call x1, Pallas kernels, last_stage(): pl.pallas_call(last_body, out_shape=jax.ShapeDtypeStruct(field.shape, jnp...  4.81 us
    reshape x2, local copies, waits for them, and re-layouts, shards(): radial_step.reshape(parts, 6, parts, 6).transpose(1, 0, 3, 2)  4.66 us
  transfers between devices with their start and end apart: 5, of which 4 were waited for; matrix products, arithmetic and copies ran while one was open for 5% of the time, Pallas kernels for 1%

profile of v2, /device:TPU:1, one launch (start us, length us, event | category | flops | bytes accessed | tf_op | source)
XLA Modules:
  0.0 219.5 jit_solution(6776364234932962673)
XLA Ops:
  0.0 5.2 %first_stage.1 = (f32[32,72,128]{2,1,0:T(8,128)}, f32[32,72,128]{2,1,0:T(8,128)}) custom-call(s32[1]{0:T(128)} %constant.76.clone.1.late_ref, f32[6,384,128]{2,1,0:T(8,128)} %bitcast.24, f32[6,384,128]{2,1,0:T(8,128)} %bitcast.27, bf16[384,384]{1,0:T(8,128)(2,1)} %constant.87.clone.th_ref, bf16[384,384]{1,0:T(8,128)(2,1)} %constant.88.clone.tl_ref, ...), custom_call_target="tpu_custom_call" | custom-call | tf_op jit(solution)/shard_map/first_filter/first_stage/pallas_call | solution.py:115
  5.2 0.0 copy-start.5
  5.2 17.1 %all-to-all-start.1 = ((f32[32,72,128]{2,1,0:T(8,128)}), f32[32,72,128]{2,1,0:T(8,128)S(1)}, u32[]{:S(2)}, u32[]{:S(2)}) async-start(f32[32,72,128]{2,1,0:T(8,128)} %get-tuple-element.8), calls=%async_computation.1 | async-start | bytes 2359296 | tf_op jit(solution)/shard_map/base_to_points/all_to_all | solution.py:208
  22.3 0.0 copy-done.5
  22.3 5.2 %collective-permute-start = (f32[32,72,128]{2,1,0:T(8,128)S(1)}, f32[32,72,128]{2,1,0:T(8,128)}, u32[]{:S(2)}, u32[]{:S(2)}) collective-permute-start(f32[32,72,128]{2,1,0:T(8,128)S(1)} %copy-done.5), channel_id=1, source_target_pairs={{480,0},{0,32},{32,64},{64,96},{96,128},{128,160},{160,192},{192,2... | collective-permute-start | bytes 3538952 | tf_op jit(solution)/shard_map/shift_state/ppermute | solution.py:56
  27.5 16.7 %collective-permute-done = f32[32,72,128]{2,1,0:T(8,128)} collective-permute-done((f32[32,72,128]{2,1,0:T(8,128)S(1)}, f32[32,72,128]{2,1,0:T(8,128)}, u32[]{:S(2)}, u32[]{:S(2)}) %collective-permute-start) | collective-permute-done | bytes 1179680 | tf_op jit(solution)/shard_map/shift_state/ppermute | solution.py:56
  44.2 36.6 %all-to-all-done.1 = f32[32,72,128]{2,1,0:T(8,128)S(1)} async-done(((f32[32,72,128]{2,1,0:T(8,128)}), f32[32,72,128]{2,1,0:T(8,128)S(1)}, u32[]{:S(2)}, u32[]{:S(2)}) %all-to-all-start.1) | async-done | bytes 1179680 | tf_op jit(solution)/shard_map/base_to_points/all_to_all | solution.py:208
  80.8 0.0 copy-start.1
  80.8 5.9 %all-to-all-start = ((f32[32,72,128]{2,1,0:T(8,128)}), f32[32,72,128]{2,1,0:T(8,128)}, u32[]{:S(2)}, u32[]{:S(2)}) async-start(f32[32,72,128]{2,1,0:T(8,128)} %collective-permute-done), calls=%async_computation | async-start | bytes 2359296 | tf_op jit(solution)/shard_map/state_to_points/all_to_all | solution.py:208
  86.7 0.0 copy-done.1
  86.7 0.0 copy-start.4
  86.7 2.6 %coefficient_stage.1 = f32[12,192,128]{2,1,0:T(8,128)} custom-call(f32[2304,128]{1,0:T(8,128)} %bitcast.26), custom_call_target="tpu_custom_call" | custom-call | tf_op jit(solution)/shard_map/shift_base/coefficient_stage/pallas_call | solution.py:144
  89.3 5.4 %collective-permute-start.1 = (f32[12,192,128]{2,1,0:T(8,128)}, f32[12,192,128]{2,1,0:T(8,128)}, u32[]{:S(2)}, u32[]{:S(2)}) collective-permute-start(f32[12,192,128]{2,1,0:T(8,128)} %coefficient_stage.1), channel_id=1, source_target_pairs={{480,0},{0,32},{32,64},{64,96},{96,128},{128,160},{160,192},{192,2... | collective-permute-start | bytes 3538952 | tf_op jit(solution)/shard_map/shift_base/ppermute | solution.py:56
  94.7 0.0 copy-done.4
  94.7 3.3 %reshape.122 = f32[32,6,32,6]{3,2,1,0:T(8,128)S(1)} reshape(f32[192,192]{1,0:T(8,128)S(1)} %copy-done.4) | data formatting | bytes 294912 | tf_op jit(solution)/shard_map/radial/reshape | solution.py:234
  98.1 2.3 %copy.15 = f32[6,32,6,32]{3,2,1,0:T(8,128)} copy(f32[6,32,6,32]{2,3,0,1:T(8,128)S(1)} %bitcast.22) | data formatting | bytes 294912 | tf_op jit(solution)/shard_map/radial/transpose | solution.py:234
  100.3 1.3 reshape.123
  101.7 0.7 fusion.1
  102.4 42.8 %all-to-all-done = f32[32,72,128]{2,1,0:T(8,128)} async-done(((f32[32,72,128]{2,1,0:T(8,128)}), f32[32,72,128]{2,1,0:T(8,128)}, u32[]{:S(2)}, u32[]{:S(2)}) %all-to-all-start) | async-done | bytes 1179680 | tf_op jit(solution)/shard_map/state_to_points/all_to_all | solution.py:208
  145.2 0.0 collective-permute-done.1.scale_ref
  145.2 4.0 %radial_stage.1 = f32[2304,128]{1,0:T(8,128)} custom-call(f32[2304,128]{1,0:T(8,128)} %bitcast.2.state_ref, f32[12,192,128]{2,1,0:T(8,128)} %collective-permute-done.1.scale_ref, bf16[192,192]{1,0:T(8,128)(2,1)} %get-tuple-element.12.high_ref, bf16[192,192]{1,0:T(8,128)(2,1)} %get-tuple-element.11.low_ref), custom_call_target="tpu_custom_call" | custom-call | tf_op jit(solution)/shard_map/radial/radial_stage/pallas_call | solution.py:174
  149.2 0.0 copy-start.3
  149.2 0.0 copy-start
  149.2 5.8 %all-to-all-start.2 = ((f32[32,72,128]{2,1,0:T(8,128)}), f32[32,72,128]{2,1,0:T(8,128)S(1)}, u32[]{:S(2)}, u32[]{:S(2)}) async-start(f32[32,72,128]{2,1,0:T(8,128)} %bitcast.23), calls=%async_computation.2 | async-start | bytes 2359296 | tf_op jit(solution)/shard_map/state_to_radii/all_to_all | solution.py:208
  157.0 0.0 copy-done.3
  157.1 0.6 gather_fusion.1
  157.7 0.1 copy.16
  157.8 0.0 copy-done
  157.9 1.7 gather_fusion
  159.6 0.6 fusion.2
  160.3 1.0 fusion
  161.3 52.3 %all-to-all-done.2.state_ref = f32[32,72,128]{2,1,0:T(8,128)S(1)} async-done(((f32[32,72,128]{2,1,0:T(8,128)}), f32[32,72,128]{2,1,0:T(8,128)S(1)}, u32[]{:S(2)}, u32[]{:S(2)}) %all-to-all-start.2) | async-done | bytes 1179680 | tf_op jit(solution)/shard_map/state_to_radii/all_to_all | solution.py:208
  213.6 0.0 copy-start.2
  213.6 1.0 copy-done.2
  214.7 4.8 %last_stage.1 = f32[6,384,128]{2,1,0:T(8,128)} custom-call(f32[32,72,128]{2,1,0:T(8,128)} %copy-done.2, f32[6,384,128]{2,1,0:T(8,128)} %bitcast.25, bf16[384,384]{1,0:T(8,128)(2,1)} %get-tuple-element.10.th_ref, bf16[384,384]{1,0:T(8,128)(2,1)} %get-tuple-element.9.tl_ref, bf16[128,128]{1,0:T(8,128)(2,1)} %get-tuple-element.14.zh_ref, ...), custom_call_target="tpu_custom_call" | custom-call | tf_op jit(solution)/shard_map/last_filter/last_stage/pallas_call | solution.py:197
  (6 shorter events, 0.1 us)
Async XLA Ops:
  5.2 17.1 %copy-start.5 = (f32[32,72,128]{2,1,0:T(8,128)S(1)}, f32[32,72,128]{2,1,0:T(8,128)}, u32[]{:S(2)}) copy-start(f32[32,72,128]{2,1,0:T(8,128)} %get-tuple-element.7) | copy-start | bytes 3538948
  5.2 75.6 %all-to-all-start.1 = ((f32[32,72,128]{2,1,0:T(8,128)}), f32[32,72,128]{2,1,0:T(8,128)S(1)}, u32[]{:S(2)}, u32[]{:S(2)}) async-start(f32[32,72,128]{2,1,0:T(8,128)} %get-tuple-element.8), calls=%async_computation.1 | async-start | bytes 2359296 | tf_op jit(solution)/shard_map/base_to_points/all_to_all | solution.py:208
  22.3 21.9 %collective-permute-start = (f32[32,72,128]{2,1,0:T(8,128)S(1)}, f32[32,72,128]{2,1,0:T(8,128)}, u32[]{:S(2)}, u32[]{:S(2)}) collective-permute-start(f32[32,72,128]{2,1,0:T(8,128)S(1)} %copy-done.5), channel_id=1, source_target_pairs={{480,0},{0,32},{32,64},{64,96},{96,128},{128,160},{160,192},{192,2... | collective-permute-start | bytes 3538952 | tf_op jit(solution)/shard_map/shift_state/ppermute | solution.py:56
  80.8 5.9 %copy-start.1 = (f32[32,72,128]{2,1,0:T(8,128)}, f32[32,72,128]{2,1,0:T(8,128)S(1)}, u32[]{:S(2)}) copy-start(f32[32,72,128]{2,1,0:T(8,128)S(1)} %all-to-all-done.1) | copy-start | bytes 3538948
  80.8 64.4 %all-to-all-start = ((f32[32,72,128]{2,1,0:T(8,128)}), f32[32,72,128]{2,1,0:T(8,128)}, u32[]{:S(2)}, u32[]{:S(2)}) async-start(f32[32,72,128]{2,1,0:T(8,128)} %collective-permute-done), calls=%async_computation | async-start | bytes 2359296 | tf_op jit(solution)/shard_map/state_to_points/all_to_all | solution.py:208
  86.7 8.0 %copy-start.4 = (f32[192,192]{1,0:T(8,128)S(1)}, f32[192,192]{1,0:T(8,128)}, u32[]{:S(2)}) copy-start(f32[192,192]{1,0:T(8,128)} %param.14) | copy-start | bytes 442372
  89.3 55.9 %collective-permute-start.1 = (f32[12,192,128]{2,1,0:T(8,128)}, f32[12,192,128]{2,1,0:T(8,128)}, u32[]{:S(2)}, u32[]{:S(2)}) collective-permute-start(f32[12,192,128]{2,1,0:T(8,128)} %coefficient_stage.1), channel_id=1, source_target_pairs={{480,0},{0,32},{32,64},{64,96},{96,128},{128,160},{160,192},{192,2... | collective-permute-start | bytes 3538952 | tf_op jit(solution)/shard_map/shift_base/ppermute | solution.py:56
  149.2 7.8 %copy-start.3 = (f32[128,128]{1,0:T(8,128)S(1)}, f32[128,128]{1,0:T(8,128)}, u32[]{:S(2)}) copy-start(f32[128,128]{1,0:T(8,128)} %constant.92.clone) | copy-start | bytes 196612
  149.2 8.6 %copy-start = (f32[384,384]{1,0:T(8,128)S(1)}, f32[384,384]{1,0:T(8,128)}, u32[]{:S(2)}) copy-start(f32[384,384]{1,0:T(8,128)} %constant.91.clone) | copy-start | bytes 1769476
  149.2 64.4 %all-to-all-start.2 = ((f32[32,72,128]{2,1,0:T(8,128)}), f32[32,72,128]{2,1,0:T(8,128)S(1)}, u32[]{:S(2)}, u32[]{:S(2)}) async-start(f32[32,72,128]{2,1,0:T(8,128)} %bitcast.23), calls=%async_computation.2 | async-start | bytes 2359296 | tf_op jit(solution)/shard_map/state_to_radii/all_to_all | solution.py:208
  213.6 1.0 copy-start.2

commit v3 on v2

--- a/solution.py
+++ b/solution.py
@@ -11,7 +11,7 @@
 
 STEP_SIZE = 0.25
 VISCOUS_RATE = 1.5e-05
-STAGGER = 0
+STAGGER = 16000
 TILE = 8
 
 

time: 222 us -> 210 us (0.946)
  Pallas kernels: 16.6 us -> 32.6 us
  waiting for transfers between devices: 148 us -> 132 us
  starting transfers between devices: 39.4 us -> 29.7 us
    all_to_all x3, waiting for transfers between devices: 132 us -> 104 us  [swap(): return lax.all_to_all(packed, 'space', 0, 0, tiled=True)]
    pallas_call x1, Pallas kernels: 5.2 us -> 21.2 us  [first_stage(): pl.pallas_call(first_body, out_shape=(shape, shape), grid=(radii // 2,),...]
    ppermute x2, waiting for transfers between devices: 16.7 us -> 28.1 us  [from_behind(): return lax.ppermute(block, axis, route)]
    ppermute x2, starting transfers between devices: 10.6 us -> 3.83 us  [from_behind(): return lax.ppermute(block, axis, route)]
    all_to_all x3, starting transfers between devices: 28.8 us -> 25.8 us  [swap(): return lax.all_to_all(packed, 'space', 0, 0, tiled=True)]
  transfers between devices with their start and end apart: 5 -> 5, of which waited for: 4 -> 5; matrix products, arithmetic and copies ran while one was open for 5% -> 6% of each run, Pallas kernels for 1% -> 1%
where the time goes in v3:
time: 210 us
  waiting for transfers between devices  132 us (63%)
  Pallas kernels  32.6 us (16%)
  starting transfers between devices  29.7 us (14%)
  local copies, waits for them, and re-layouts  10.4 us (5%)
  other arithmetic  2.46 us (1%)
  between operations  2.12 us (1%)
    all_to_all x3, waiting for transfers between devices, swap(): return lax.all_to_all(packed, 'space', 0, 0, tiled=True)  104 us
    ppermute x2, waiting for transfers between devices, from_behind(): return lax.ppermute(block, axis, route)  28.1 us
    all_to_all x3, starting transfers between devices, swap(): return lax.all_to_all(packed, 'space', 0, 0, tiled=True)  25.8 us
    pallas_call x1, Pallas kernels, first_stage(): pl.pallas_call(first_body, out_shape=(shape, shape), grid=(radii // 2,),...  21.2 us
    pallas_call x1, Pallas kernels, last_stage(): pl.pallas_call(last_body, out_shape=jax.ShapeDtypeStruct(field.shape, jnp...  4.81 us
    reshape x2, local copies, waits for them, and re-layouts, shards(): radial_step.reshape(parts, 6, parts, 6).transpose(1, 0, 3, 2)  4.66 us
  transfers between devices with their start and end apart: 5, of which 5 were waited for; matrix products, arithmetic and copies ran while one was open for 6% of the time, Pallas kernels for 1%

profile of v3, /device:TPU:1, one launch (start us, length us, event | category | flops | bytes accessed | tf_op | source)
XLA Modules:
  0.0 209.6 jit_solution(15388606479738960111)
XLA Ops:
  0.0 21.2 %first_stage.1 = (f32[32,72,128]{2,1,0:T(8,128)}, f32[32,72,128]{2,1,0:T(8,128)}) custom-call(s32[1]{0:T(128)} %bitcast.late_ref, f32[6,384,128]{2,1,0:T(8,128)} %bitcast.25, f32[6,384,128]{2,1,0:T(8,128)} %bitcast.28, bf16[384,384]{1,0:T(8,128)(2,1)} %constant.96.clone.th_ref, bf16[384,384]{1,0:T(8,128)(2,1)} %constant.97.clone.tl_ref, ...), custom_call_target="tpu_custom_call" | custom-call | tf_op jit(solution)/shard_map/first_filter/first_stage/pallas_call | solution.py:115
  21.2 0.0 copy-start.5
  21.2 17.1 %all-to-all-start.1 = ((f32[32,72,128]{2,1,0:T(8,128)}), f32[32,72,128]{2,1,0:T(8,128)S(1)}, u32[]{:S(2)}, u32[]{:S(2)}) async-start(f32[32,72,128]{2,1,0:T(8,128)} %get-tuple-element.8), calls=%async_computation.1 | async-start | bytes 2359296 | tf_op jit(solution)/shard_map/base_to_points/all_to_all | solution.py:208
  38.3 0.0 copy-done.5
  38.3 1.9 collective-permute-start
  40.2 18.1 %collective-permute-done = f32[32,72,128]{2,1,0:T(8,128)} collective-permute-done((f32[32,72,128]{2,1,0:T(8,128)S(1)}, f32[32,72,128]{2,1,0:T(8,128)}, u32[]{:S(2)}, u32[]{:S(2)}) %collective-permute-start) | collective-permute-done | bytes 1179680 | tf_op jit(solution)/shard_map/shift_state/ppermute | solution.py:56
  58.4 26.6 %all-to-all-done.1 = f32[32,72,128]{2,1,0:T(8,128)S(1)} async-done(((f32[32,72,128]{2,1,0:T(8,128)}), f32[32,72,128]{2,1,0:T(8,128)S(1)}, u32[]{:S(2)}, u32[]{:S(2)}) %all-to-all-start.1) | async-done | bytes 1179680 | tf_op jit(solution)/shard_map/base_to_points/all_to_all | solution.py:208
  85.0 0.0 copy-start.1
  85.0 4.7 %all-to-all-start = ((f32[32,72,128]{2,1,0:T(8,128)}), f32[32,72,128]{2,1,0:T(8,128)}, u32[]{:S(2)}, u32[]{:S(2)}) async-start(f32[32,72,128]{2,1,0:T(8,128)} %collective-permute-done), calls=%async_computation | async-start | bytes 2359296 | tf_op jit(solution)/shard_map/state_to_points/all_to_all | solution.py:208
  89.7 0.0 copy-done.1
  89.7 0.0 copy-start.4
  89.7 2.6 %coefficient_stage.1 = f32[12,192,128]{2,1,0:T(8,128)} custom-call(f32[2304,128]{1,0:T(8,128)} %bitcast.27), custom_call_target="tpu_custom_call" | custom-call | tf_op jit(solution)/shard_map/shift_base/coefficient_stage/pallas_call | solution.py:144
  92.3 1.9 collective-permute-start.1
  94.2 0.0 copy-done.4
  94.3 3.3 %reshape.122 = f32[32,6,32,6]{3,2,1,0:T(8,128)S(1)} reshape(f32[192,192]{1,0:T(8,128)S(1)} %copy-done.4) | data formatting | bytes 294912 | tf_op jit(solution)/shard_map/radial/reshape | solution.py:234
  97.6 2.3 %copy.15 = f32[6,32,6,32]{3,2,1,0:T(8,128)} copy(f32[6,32,6,32]{2,3,0,1:T(8,128)S(1)} %bitcast.23) | data formatting | bytes 294912 | tf_op jit(solution)/shard_map/radial/transpose | solution.py:234
  99.8 1.3 reshape.123
  101.2 0.7 fusion.1
  101.9 10.0 %collective-permute-done.1.scale_ref = f32[12,192,128]{2,1,0:T(8,128)} collective-permute-done((f32[12,192,128]{2,1,0:T(8,128)}, f32[12,192,128]{2,1,0:T(8,128)}, u32[]{:S(2)}, u32[]{:S(2)}) %collective-permute-start.1) | collective-permute-done | bytes 1179680 | tf_op jit(solution)/shard_map/shift_base/ppermute | solution.py:56
  111.8 28.7 %all-to-all-done = f32[32,72,128]{2,1,0:T(8,128)} async-done(((f32[32,72,128]{2,1,0:T(8,128)}), f32[32,72,128]{2,1,0:T(8,128)}, u32[]{:S(2)}, u32[]{:S(2)}) %all-to-all-start) | async-done | bytes 1179680 | tf_op jit(solution)/shard_map/state_to_points/all_to_all | solution.py:208
  140.5 4.0 %radial_stage.1 = f32[2304,128]{1,0:T(8,128)} custom-call(f32[2304,128]{1,0:T(8,128)} %bitcast.3.state_ref, f32[12,192,128]{2,1,0:T(8,128)} %collective-permute-done.1.scale_ref, bf16[192,192]{1,0:T(8,128)(2,1)} %get-tuple-element.12.high_ref, bf16[192,192]{1,0:T(8,128)(2,1)} %get-tuple-element.11.low_ref), custom_call_target="tpu_custom_call" | custom-call | tf_op jit(solution)/shard_map/radial/radial_stage/pallas_call | solution.py:174
  144.5 0.0 copy-start.3
  144.5 0.0 copy-start
  144.5 4.1 %all-to-all-start.2 = ((f32[32,72,128]{2,1,0:T(8,128)}), f32[32,72,128]{2,1,0:T(8,128)S(1)}, u32[]{:S(2)}, u32[]{:S(2)}) async-start(f32[32,72,128]{2,1,0:T(8,128)} %bitcast.24), calls=%async_computation.2 | async-start | bytes 2359296 | tf_op jit(solution)/shard_map/state_to_radii/all_to_all | solution.py:208
  150.6 0.0 copy-done.3
  150.6 0.6 gather_fusion.1
  151.3 0.1 copy.16
  151.4 0.0 copy-done
  151.4 1.7 gather_fusion
  153.2 0.6 fusion.2
  153.9 1.0 fusion
  154.9 48.9 %all-to-all-done.2.state_ref = f32[32,72,128]{2,1,0:T(8,128)S(1)} async-done(((f32[32,72,128]{2,1,0:T(8,128)}), f32[32,72,128]{2,1,0:T(8,128)S(1)}, u32[]{:S(2)}, u32[]{:S(2)}) %all-to-all-start.2) | async-done | bytes 1179680 | tf_op jit(solution)/shard_map/state_to_radii/all_to_all | solution.py:208
  203.8 0.0 copy-start.2
  203.8 1.0 copy-done.2
  204.8 4.8 %last_stage.1 = f32[6,384,128]{2,1,0:T(8,128)} custom-call(f32[32,72,128]{2,1,0:T(8,128)} %copy-done.2, f32[6,384,128]{2,1,0:T(8,128)} %bitcast.26, bf16[384,384]{1,0:T(8,128)(2,1)} %get-tuple-element.10.th_ref, bf16[384,384]{1,0:T(8,128)(2,1)} %get-tuple-element.9.tl_ref, bf16[128,128]{1,0:T(8,128)(2,1)} %get-tuple-element.14.zh_ref, ...), custom_call_target="tpu_custom_call" | custom-call | tf_op jit(solution)/shard_map/last_filter/last_stage/pallas_call | solution.py:197
  (6 shorter events, 0.1 us)
Async XLA Ops:
  21.2 17.1 %copy-start.5 = (f32[32,72,128]{2,1,0:T(8,128)S(1)}, f32[32,72,128]{2,1,0:T(8,128)}, u32[]{:S(2)}) copy-start(f32[32,72,128]{2,1,0:T(8,128)} %get-tuple-element.7) | copy-start | bytes 3538948
  21.2 63.8 %all-to-all-start.1 = ((f32[32,72,128]{2,1,0:T(8,128)}), f32[32,72,128]{2,1,0:T(8,128)S(1)}, u32[]{:S(2)}, u32[]{:S(2)}) async-start(f32[32,72,128]{2,1,0:T(8,128)} %get-tuple-element.8), calls=%async_computation.1 | async-start | bytes 2359296 | tf_op jit(solution)/shard_map/base_to_points/all_to_all | solution.py:208
  38.3 20.1 %collective-permute-start = (f32[32,72,128]{2,1,0:T(8,128)S(1)}, f32[32,72,128]{2,1,0:T(8,128)}, u32[]{:S(2)}, u32[]{:S(2)}) collective-permute-start(f32[32,72,128]{2,1,0:T(8,128)S(1)} %copy-done.5), channel_id=1, source_target_pairs={{480,0},{0,32},{32,64},{64,96},{96,128},{128,160},{160,192},{192,2... | collective-permute-start | bytes 3538952 | tf_op jit(solution)/shard_map/shift_state/ppermute | solution.py:56
  85.0 4.7 %copy-start.1 = (f32[32,72,128]{2,1,0:T(8,128)}, f32[32,72,128]{2,1,0:T(8,128)S(1)}, u32[]{:S(2)}) copy-start(f32[32,72,128]{2,1,0:T(8,128)S(1)} %all-to-all-done.1) | copy-start | bytes 3538948
  85.0 55.5 %all-to-all-start = ((f32[32,72,128]{2,1,0:T(8,128)}), f32[32,72,128]{2,1,0:T(8,128)}, u32[]{:S(2)}, u32[]{:S(2)}) async-start(f32[32,72,128]{2,1,0:T(8,128)} %collective-permute-done), calls=%async_computation | async-start | bytes 2359296 | tf_op jit(solution)/shard_map/state_to_points/all_to_all | solution.py:208
  89.7 4.5 %copy-start.4 = (f32[192,192]{1,0:T(8,128)S(1)}, f32[192,192]{1,0:T(8,128)}, u32[]{:S(2)}) copy-start(f32[192,192]{1,0:T(8,128)} %param.14) | copy-start | bytes 442372
  92.3 19.5 %collective-permute-start.1 = (f32[12,192,128]{2,1,0:T(8,128)}, f32[12,192,128]{2,1,0:T(8,128)}, u32[]{:S(2)}, u32[]{:S(2)}) collective-permute-start(f32[12,192,128]{2,1,0:T(8,128)} %coefficient_stage.1), channel_id=1, source_target_pairs={{480,0},{0,32},{32,64},{64,96},{96,128},{128,160},{160,192},{192,2... | collective-permute-start | bytes 3538952 | tf_op jit(solution)/shard_map/shift_base/ppermute | solution.py:56
  144.5 6.1 %copy-start.3 = (f32[128,128]{1,0:T(8,128)S(1)}, f32[128,128]{1,0:T(8,128)}, u32[]{:S(2)}) copy-start(f32[128,128]{1,0:T(8,128)} %constant.101.clone) | copy-start | bytes 196612
  144.5 6.9 %copy-start = (f32[384,384]{1,0:T(8,128)S(1)}, f32[384,384]{1,0:T(8,128)}, u32[]{:S(2)}) copy-start(f32[384,384]{1,0:T(8,128)} %constant.100.clone) | copy-start | bytes 1769476
  144.5 59.2 %all-to-all-start.2 = ((f32[32,72,128]{2,1,0:T(8,128)}), f32[32,72,128]{2,1,0:T(8,128)S(1)}, u32[]{:S(2)}, u32[]{:S(2)}) async-start(f32[32,72,128]{2,1,0:T(8,128)} %bitcast.24), calls=%async_computation.2 | async-start | bytes 2359296 | tf_op jit(solution)/shard_map/state_to_radii/all_to_all | solution.py:208
  203.8 1.0 copy-start.2

commit v4 on v3

--- a/solution.py
+++ b/solution.py
@@ -11,7 +11,7 @@
 
 STEP_SIZE = 0.25
 VISCOUS_RATE = 1.5e-05
-STAGGER = 16000
+STAGGER = 20000
 TILE = 8
 
 
@@ -87,39 +87,51 @@
 
 def filter_pair(first, second, table_t, table_z):
     count_z = first.shape[1]
-    first = product(split(first), table_z)
-    second = product(split(second), table_z)
-    both = product(table_t, split(jnp.concatenate([first, second], 1)))
+    both = product(split(jnp.concatenate([first, second], 1)), table_z)
+    both = product(table_t, split(both))
     return both[:, :count_z], both[:, count_z:]
 
 
-def first_body(late_ref, field_ref, base_ref, th_ref, tl_ref, zh_ref, zl_ref, state_ref, base_out_ref):
+def first_body(field_ref, base_ref, th_ref, tl_ref, zh_ref, zl_ref, state_ref, base_out_ref):
     pack_pair(base_out_ref, base_ref[0], base_ref[1])
     forced = [field_ref[k] + STEP_SIZE * base_ref[k] * field_ref[k] for k in range(2)]
     table_t = (th_ref[...], tl_ref[...])
     table_z = (zh_ref[...], zl_ref[...])
     pack_pair(state_ref, *filter_pair(*forced, table_t, table_z))
 
-    @pl.when(pl.program_id(0) == pl.num_programs(0) - 1)
-    def _():
-        pl.delay(late_ref[0])
-
-
-def first_stage(field, base, table_t, table_z, parts, late):
+
+def first_stage(field, base, table_t, table_z, parts):
     radii, count_t, count_z = field.shape
     plane = pl.BlockSpec((2, count_t, count_z), lambda p: (p, 0, 0))
     packed = pl.BlockSpec((parts, 24, count_z), lambda p: (0, p, 0))
     whole_t = pl.BlockSpec((count_t, count_t), lambda p: (0, 0))
-    whole_z = pl.BlockSpec((count_z, count_z), lambda p: (0, 0))
+    whole_z = pl.BlockSpec((2 * count_z, 2 * count_z), lambda p: (0, 0))
     shape = jax.ShapeDtypeStruct((parts, 12 * radii, count_z), jnp.float32)
     return pl.pallas_call(
         first_body,
         out_shape=(shape, shape),
         grid=(radii // 2,),
-        in_specs=[pl.BlockSpec(memory_space=pltpu.SMEM), plane, plane, whole_t, whole_t, whole_z, whole_z],
+        in_specs=[plane, plane, whole_t, whole_t, whole_z, whole_z],
         out_specs=(packed, packed),
         name="first_stage",
-    )(late, field, base, *table_t, *table_z)
+    )(field, base, *table_t, *table_z)
+
+
+def hold_body(late_ref, block_ref, out_ref):
+    pl.delay(late_ref[0])
+
+
+def hold(block, late, weight):
+    whole = pl.BlockSpec(memory_space=pl.ANY)
+    return pl.pallas_call(
+        hold_body,
+        out_shape=jax.ShapeDtypeStruct(block.shape, block.dtype),
+        in_specs=[pl.BlockSpec(memory_space=pltpu.SMEM), whole],
+        out_specs=whole,
+        input_output_aliases={1: 0},
+        cost_estimate=pl.CostEstimate(flops=weight * 1000, transcendentals=0, bytes_accessed=0),
+        name="hold",
+    )(late, block)
 
 
 def row_of(pair, half, point):
@@ -177,31 +189,53 @@
         in_specs=[vmem] * 4,
         out_specs=vmem,
         name="radial_stage",
-    )(state, scale, *mix)
-
-
-def last_body(state_ref, field_ref, th_ref, tl_ref, zh_ref, zl_ref, out_ref):
+    )(*in_vmem(state, scale, *mix))
+
+
+def last_body(state_ref, field_ref, th_ref, tl_ref, zh_ref, zl_ref, out_ref, start, buffer, start_sems, sems):
     table_t = (th_ref[...], tl_ref[...])
     table_z = (zh_ref[...], zl_ref[...])
-    first, second = filter_pair(*unpack_pair(state_ref), table_t, table_z)
-    out_ref[0] = first - field_ref[0]
-    out_ref[1] = second - field_ref[1]
-
-
-def last_stage(state, field, table_t, table_z, parts):
-    radii, count_t, count_z = field.shape
-    plane = pl.BlockSpec((2, count_t, count_z), lambda p: (p, 0, 0))
-    packed = pl.BlockSpec((parts, 24, count_z), lambda p: (0, p, 0))
-    whole_t = pl.BlockSpec((count_t, count_t), lambda p: (0, 0))
-    whole_z = pl.BlockSpec((count_z, count_z), lambda p: (0, 0))
+    pairs = start.shape[0] // 2
+    rows = 12 * start.shape[0]
+    state_ref = state_ref.reshape(state_ref.shape[0] // rows, rows, state_ref.shape[1])
+    loads, copies = [], []
+    for pair in range(pairs):
+        planes = pl.ds(2 * pair, 2)
+        loads.append(pltpu.make_async_copy(field_ref.at[planes], start.at[planes], start_sems.at[pair]))
+        loads[-1].start()
+    for pair in range(pairs):
+        planes = pl.ds(2 * pair, 2)
+        first, second = filter_pair(*unpack_pair(state_ref.at[:, pl.ds(24 * pair, 24), :]), table_t, table_z)
+        loads[pair].wait()
+        buffer[2 * pair] = first - start[2 * pair]
+        buffer[2 * pair + 1] = second - start[2 * pair + 1]
+        copies.append(pltpu.make_async_copy(buffer.at[planes], out_ref.at[planes], sems.at[pair]))
+        copies[-1].start()
+    for copy in copies:
+        copy.wait()
+
+
+def in_vmem(*arrays):
+    return [pltpu.with_memory_space_constraint(array, pltpu.VMEM) for array in arrays]
+
+
+def last_stage(state, field, table_t, table_z):
+    vmem = pl.BlockSpec(memory_space=pltpu.VMEM)
+    whole = pl.BlockSpec(memory_space=pl.ANY)
+    (state,) = in_vmem(state)
     return pl.pallas_call(
         last_body,
         out_shape=jax.ShapeDtypeStruct(field.shape, jnp.float32),
-        grid=(radii // 2,),
-        in_specs=[packed, plane, whole_t, whole_t, whole_z, whole_z],
-        out_specs=plane,
+        in_specs=[vmem, whole, vmem, vmem, vmem, vmem],
+        out_specs=whole,
+        scratch_shapes=[
+            pltpu.VMEM(field.shape, jnp.float32),
+            pltpu.VMEM(field.shape, jnp.float32),
+            pltpu.SemaphoreType.DMA((field.shape[0] // 2,)),
+            pltpu.SemaphoreType.DMA((field.shape[0] // 2,)),
+        ],
         name="last_stage",
-    )(state, field, *table_t, *table_z)
+    )(state, field, *in_vmem(*table_t, *table_z))
 
 
 def swap(packed):
@@ -216,15 +250,17 @@
     table_t = filter_table(count_t)
     table_z = filter_table(count_z)
 
-    late = (STAGGER * (segment % 2)).astype(jnp.int32)[None]
+    late = (STAGGER * ((segment + 1) // 2 % 2)).astype(jnp.int32)[None]
     with jax.named_scope("first_filter"):
+        pair_z = np.kron(np.eye(2, dtype=np.float32), table_z)
         filtered, base_packed = first_stage(
-            state, base[0], split_constant(table_t), split_constant(table_z), parts, late
+            state, base[0], split_constant(table_t), split_constant(pair_z), parts
         )
     with jax.named_scope("shift_state"):
         filtered = from_behind(filtered, "seg", 1)
+        filtered = hold(filtered, jnp.zeros_like(late), 1 << 30)
     with jax.named_scope("base_to_points"):
-        base_points = swap(base_packed)
+        base_points = swap(hold(base_packed, late, 0))
     with jax.named_scope("shift_base"):
         scale = coefficient_stage(base_points.reshape(-1, count_z), parts)
         scale = from_behind(scale, "seg", 1)
@@ -243,9 +279,10 @@
         index_t = jnp.where(closing, (az_shift[0] - places_t) % count_t, places_t)
         index_z = jnp.where(closing, (places_z + ax_shift[0]) % count_z, places_z)
         last_t = split_array(jnp.take(jnp.asarray(table_t), index_t, axis=0))
-        last_z = split_array(jnp.take(jnp.asarray(table_z), index_z, axis=0).T)
+        last_z = jnp.take(jnp.asarray(table_z), index_z, axis=0).T
+        last_z = split_array(jnp.kron(jnp.eye(2, dtype=jnp.float32), last_z))
     with jax.named_scope("last_filter"):
-        return last_stage(carried, state, last_t, last_z, parts)[None]
+        return last_stage(carried.reshape(-1, count_z), state, last_t, last_z)[None]
 
 
 def solution(mesh):

time: 210 us -> 196 us (0.933)
  starting transfers between devices: 29.7 us -> 53.3 us
  waiting for transfers between devices: 132 us -> 112 us
  Pallas kernels: 32.6 us -> 15.7 us
    ppermute x2, waiting for transfers between devices: 28.1 us -> 8.76 us  [from_behind(): return lax.ppermute(block, axis, route)]
    all_to_all x3, starting transfers between devices: 25.8 us -> 44.8 us  [swap(): return lax.all_to_all(packed, 'space', 0, 0, tiled=True)]
    pallas_call x1, Pallas kernels: 21.2 us -> 5.82 us  [first_stage(): pl.pallas_call(first_body, out_shape=(shape, shape), grid=(radii // 2,),...]
    ppermute x2, starting transfers between devices: 3.83 us -> 8.5 us  [from_behind(): return lax.ppermute(block, axis, route)]
    convert_element_type x3, other arithmetic: 2.36 us -> 0.22 us  [split_array(): return (high.astype(jnp.bfloat16), (array - high).astype(jnp.bfloat16))]
  transfers between devices with their start and end apart: 5 -> 5, of which waited for: 5 -> 4; matrix products, arithmetic and copies ran while one was open for 6% -> 6% of each run, Pallas kernels for 1% -> 1%
where the time goes in v4:
time: 196 us; the launch traced here: 195 us
  waiting for transfers between devices  112 us (57%)
  starting transfers between devices  53.3 us (27%)
  Pallas kernels  15.7 us (8%)
  local copies, waits for them, and re-layouts  11.4 us (6%)
  between operations  2.18 us (1%)
    all_to_all x3, waiting for transfers between devices, swap(): return lax.all_to_all(packed, 'space', 0, 0, tiled=True)  103 us
    all_to_all x3, starting transfers between devices, swap(): return lax.all_to_all(packed, 'space', 0, 0, tiled=True)  44.8 us
    ppermute x2, waiting for transfers between devices, from_behind(): return lax.ppermute(block, axis, route)  8.76 us
    ppermute x2, starting transfers between devices, from_behind(): return lax.ppermute(block, axis, route)  8.5 us
    pallas_call x1, Pallas kernels, first_stage(): pl.pallas_call(first_body, out_shape=(shape, shape), grid=(radii // 2,),...  5.82 us
    reshape x2, local copies, waits for them, and re-layouts, shards(): radial_step.reshape(parts, 6, parts, 6).transpose(1, 0, 3, 2)  5.18 us
    pallas_call x1, Pallas kernels, last_stage(): pl.pallas_call(last_body, out_shape=jax.ShapeDtypeStruct(field.shape, jnp...  4.9 us
  transfers between devices with their start and end apart: 5, of which 4 were waited for; matrix products, arithmetic and copies ran while one was open for 6% of the time, Pallas kernels for 1%

profile of v4, /device:TPU:1, one launch (start us, length us, event | category | flops | bytes accessed | tf_op | source)
XLA Modules:
  0.0 194.8 jit_solution(1148492320120836136)
XLA Ops:
  0.0 5.8 %first_stage.1 = (f32[32,72,128]{2,1,0:T(8,128)}, f32[32,72,128]{2,1,0:T(8,128)}) custom-call(f32[6,384,128]{2,1,0:T(8,128)} %bitcast.32, f32[6,384,128]{2,1,0:T(8,128)} %bitcast.34, bf16[384,384]{1,0:T(8,128)(2,1)} %constant.110.clone.th_ref, bf16[384,384]{1,0:T(8,128)(2,1)} %constant.111.clone.tl_ref, bf16[256,256]{1,0:T(8,128)(2,1)} %constant.112.clone.zh_ref, ...), custom_call_target="tpu_custom_call" | custom-call | tf_op jit(solution)/shard_map/first_filter/first_stage/pallas_call | solution.py:110
  5.8 6.0 %collective-permute-start = (f32[32,72,128]{2,1,0:T(8,128)}, f32[32,72,128]{2,1,0:T(8,128)S(1)}, u32[]{:S(2)}, u32[]{:S(2)}) collective-permute-start(f32[32,72,128]{2,1,0:T(8,128)} %get-tuple-element.7), channel_id=1, source_target_pairs={{480,0},{0,32},{32,64},{64,96},{96,128},{128,160},{160,192},{192,2... | collective-permute-start | bytes 3538952 | tf_op jit(solution)/shard_map/shift_state/ppermute | solution.py:56
  11.9 35.3 %all-to-all-start.1 = ((f32[32,72,128]{2,1,0:T(8,128)}), f32[32,72,128]{2,1,0:T(8,128)}, u32[]{:S(2)}, u32[]{:S(2)}) async-start(f32[32,72,128]{2,1,0:T(8,128)} %hold.3), calls=%async_computation.1 | async-start | bytes 2359296 | tf_op jit(solution)/shard_map/base_to_points/all_to_all | solution.py:242
  47.2 0.0 collective-permute-done.block_ref
  47.3 0.0 copy-start.2
  47.3 1.0 copy-done.2
  48.3 42.7 %all-to-all-done.1 = f32[32,72,128]{2,1,0:T(8,128)} async-done(((f32[32,72,128]{2,1,0:T(8,128)}), f32[32,72,128]{2,1,0:T(8,128)}, u32[]{:S(2)}, u32[]{:S(2)}) %all-to-all-start.1) | async-done | bytes 1179680 | tf_op jit(solution)/shard_map/base_to_points/all_to_all | solution.py:242
  91.0 5.4 %all-to-all-start = ((f32[32,72,128]{2,1,0:T(8,128)}), f32[32,72,128]{2,1,0:T(8,128)S(1)}, u32[]{:S(2)}, u32[]{:S(2)}) async-start(f32[32,72,128]{2,1,0:T(8,128)} %hold.2), calls=%async_computation | async-start | bytes 2359296 | tf_op jit(solution)/shard_map/state_to_points/all_to_all | solution.py:242
  96.4 0.0 copy-start.3
  96.4 2.6 %coefficient_stage.1 = f32[12,192,128]{2,1,0:T(8,128)} custom-call(f32[2304,128]{1,0:T(8,128)} %bitcast.4.base_ref), custom_call_target="tpu_custom_call" | custom-call | tf_op jit(solution)/shard_map/shift_base/coefficient_stage/pallas_call | solution.py:156
  99.0 2.5 %collective-permute-start.1 = (f32[12,192,128]{2,1,0:T(8,128)}, f32[12,192,128]{2,1,0:T(8,128)S(1)}, u32[]{:S(2)}, u32[]{:S(2)}) collective-permute-start(f32[12,192,128]{2,1,0:T(8,128)} %coefficient_stage.1), channel_id=1, source_target_pairs={{480,0},{0,32},{32,64},{64,96},{96,128},{128,160},{160,192},{192,2... | collective-permute-start | bytes 3538952 | tf_op jit(solution)/shard_map/shift_base/ppermute | solution.py:56
  101.5 0.0 copy-done.3
  101.5 5.0 %reshape.139 = f32[32,6,32,6]{3,2,1,0:T(8,128)} reshape(f32[192,192]{1,0:T(8,128)S(1)} %copy-done.3) | data formatting | bytes 294912 | tf_op jit(solution)/shard_map/radial/reshape | solution.py:270
  106.5 2.7 %copy.17 = f32[6,32,6,32]{3,2,1,0:T(8,128)S(1)} copy(f32[6,32,6,32]{2,3,0,1:T(8,128)} %bitcast.30) | data formatting | bytes 294912 | tf_op jit(solution)/shard_map/radial/transpose | solution.py:270
  109.2 0.2 reshape.140
  109.5 8.8 %collective-permute-done.1.scale_ref = f32[12,192,128]{2,1,0:T(8,128)S(1)} collective-permute-done((f32[12,192,128]{2,1,0:T(8,128)}, f32[12,192,128]{2,1,0:T(8,128)S(1)}, u32[]{:S(2)}, u32[]{:S(2)}) %collective-permute-start.1) | collective-permute-done | bytes 1179680 | tf_op jit(solution)/shard_map/shift_base/ppermute | solution.py:56
  118.2 19.8 %all-to-all-done = f32[32,72,128]{2,1,0:T(8,128)S(1)} async-done(((f32[32,72,128]{2,1,0:T(8,128)}), f32[32,72,128]{2,1,0:T(8,128)S(1)}, u32[]{:S(2)}, u32[]{:S(2)}) %all-to-all-start) | async-done | bytes 1179680 | tf_op jit(solution)/shard_map/state_to_points/all_to_all | solution.py:242
  138.0 2.4 %radial_stage.1 = f32[2304,128]{1,0:T(8,128)} custom-call(f32[2304,128]{1,0:T(8,128)S(1)} %bitcast.28, f32[12,192,128]{2,1,0:T(8,128)S(1)} %collective-permute-done.1.scale_ref, bf16[192,192]{1,0:T(8,128)(2,1)S(1)} %get-tuple-element.14.high_ref, bf16[192,192]{1,0:T(8,128)(2,1)S(1)} %get-tuple-element.13.low_ref), custom_call_target="tpu_custom_call" | custom-call | tf_op jit(solution)/shard_map/radial/radial_stage/pallas_call | solution.py:186
  140.4 0.0 copy-start.1
  140.4 0.0 copy-start
  140.5 4.1 %all-to-all-start.2 = ((f32[32,72,128]{2,1,0:T(8,128)}), f32[32,72,128]{2,1,0:T(8,128)S(1)}, u32[]{:S(2)}, u32[]{:S(2)}) async-start(f32[32,72,128]{2,1,0:T(8,128)} %bitcast.31), calls=%async_computation.2 | async-start | bytes 2359296 | tf_op jit(solution)/shard_map/state_to_radii/all_to_all | solution.py:242
  146.5 0.0 copy-done.1
  146.5 0.6 gather_fusion.1
  147.2 0.1 select_bitcast_fusion
  147.3 0.1 copy.18
  147.4 0.0 copy-done
  147.4 1.7 gather_fusion
  149.2 0.1 broadcast_multiply_fusion
  149.4 0.2 fusion
  149.6 40.3 %all-to-all-done.2 = f32[32,72,128]{2,1,0:T(8,128)S(1)} async-done(((f32[32,72,128]{2,1,0:T(8,128)}), f32[32,72,128]{2,1,0:T(8,128)S(1)}, u32[]{:S(2)}, u32[]{:S(2)}) %all-to-all-start.2) | async-done | bytes 1179680 | tf_op jit(solution)/shard_map/state_to_radii/all_to_all | solution.py:242
  189.9 4.9 %last_stage.1 = f32[6,384,128]{2,1,0:T(8,128)} custom-call(f32[2304,128]{1,0:T(8,128)S(1)} %bitcast.29, f32[6,384,128]{2,1,0:T(8,128)} %bitcast.33, bf16[384,384]{1,0:T(8,128)(2,1)S(1)} %get-tuple-element.10.th_ref, bf16[384,384]{1,0:T(8,128)(2,1)S(1)} %get-tuple-element.9.tl_ref, bf16[256,256]{1,0:T(8,128)(2,1)S(1)} %get-tuple-element.12.zh_ref, ...), custom_call_target="tpu_custom_call" | custom-call | tf_op jit(solution)/shard_map/last_filter/last_stage/pallas_call | solution.py:226
  (11 shorter events, 0.2 us)
Async XLA Ops:
  5.8 41.4 %collective-permute-start = (f32[32,72,128]{2,1,0:T(8,128)}, f32[32,72,128]{2,1,0:T(8,128)S(1)}, u32[]{:S(2)}, u32[]{:S(2)}) collective-permute-start(f32[32,72,128]{2,1,0:T(8,128)} %get-tuple-element.7), channel_id=1, source_target_pairs={{480,0},{0,32},{32,64},{64,96},{96,128},{128,160},{160,192},{192,2... | collective-permute-start | bytes 3538952 | tf_op jit(solution)/shard_map/shift_state/ppermute | solution.py:56
  11.9 79.1 %all-to-all-start.1 = ((f32[32,72,128]{2,1,0:T(8,128)}), f32[32,72,128]{2,1,0:T(8,128)}, u32[]{:S(2)}, u32[]{:S(2)}) async-start(f32[32,72,128]{2,1,0:T(8,128)} %hold.3), calls=%async_computation.1 | async-start | bytes 2359296 | tf_op jit(solution)/shard_map/base_to_points/all_to_all | solution.py:242
  47.3 1.0 copy-start.2
  91.0 47.1 %all-to-all-start = ((f32[32,72,128]{2,1,0:T(8,128)}), f32[32,72,128]{2,1,0:T(8,128)S(1)}, u32[]{:S(2)}, u32[]{:S(2)}) async-start(f32[32,72,128]{2,1,0:T(8,128)} %hold.2), calls=%async_computation | async-start | bytes 2359296 | tf_op jit(solution)/shard_map/state_to_points/all_to_all | solution.py:242
  96.4 5.1 %copy-start.3 = (f32[192,192]{1,0:T(8,128)S(1)}, f32[192,192]{1,0:T(8,128)}, u32[]{:S(2)}) copy-start(f32[192,192]{1,0:T(8,128)} %param.14) | copy-start | bytes 442372
  99.0 19.2 %collective-permute-start.1 = (f32[12,192,128]{2,1,0:T(8,128)}, f32[12,192,128]{2,1,0:T(8,128)S(1)}, u32[]{:S(2)}, u32[]{:S(2)}) collective-permute-start(f32[12,192,128]{2,1,0:T(8,128)} %coefficient_stage.1), channel_id=1, source_target_pairs={{480,0},{0,32},{32,64},{64,96},{96,128},{128,160},{160,192},{192,2... | collective-permute-start | bytes 3538952 | tf_op jit(solution)/shard_map/shift_base/ppermute | solution.py:56
  140.4 6.1 %copy-start.1 = (f32[128,128]{1,0:T(8,128)S(1)}, f32[128,128]{1,0:T(8,128)}, u32[]{:S(2)}) copy-start(f32[128,128]{1,0:T(8,128)} %constant.115.clone) | copy-start | bytes 196612
  140.4 7.0 %copy-start = (f32[384,384]{1,0:T(8,128)S(1)}, f32[384,384]{1,0:T(8,128)}, u32[]{:S(2)}) copy-start(f32[384,384]{1,0:T(8,128)} %constant.114.clone) | copy-start | bytes 1769476
  140.5 49.5 %all-to-all-start.2 = ((f32[32,72,128]{2,1,0:T(8,128)}), f32[32,72,128]{2,1,0:T(8,128)S(1)}, u32[]{:S(2)}, u32[]{:S(2)}) async-start(f32[32,72,128]{2,1,0:T(8,128)} %bitcast.31), calls=%async_computation.2 | async-start | bytes 2359296 | tf_op jit(solution)/shard_map/state_to_radii/all_to_all | solution.py:242

commit v5 on v4

--- a/solution.py
+++ b/solution.py
@@ -11,7 +11,7 @@
 
 STEP_SIZE = 0.25
 VISCOUS_RATE = 1.5e-05
-STAGGER = 20000
+STAGGER = 22000
 TILE = 8
 
 
@@ -23,10 +23,16 @@
     scale = np.where(rows < 2, math.sqrt(1.0 / size), math.sqrt(2.0 / size))
     table = scale[:, None] * np.where(sine[:, None], np.sin(angle), np.cos(angle))
     decay = np.exp(-VISCOUS_RATE * wave.astype(np.float64) ** 2)
-    return (table.T @ (decay[:, None] * table)).astype(np.float32)
+    return table.T @ (decay[:, None] * table)
+
+
+def halves(table):
+    half = table.shape[0] // 2
+    return np.concatenate([table[:, :half] + table[:, half:], table[:, :half] - table[:, half:]], 0) / 2
 
 
 def split_constant(table):
+    table = table.astype(np.float32)
     high = table.astype(ml_dtypes.bfloat16)
     return high, (table - high.astype(np.float32)).astype(ml_dtypes.bfloat16)
 
@@ -87,8 +93,11 @@
 
 def filter_pair(first, second, table_t, table_z):
     count_z = first.shape[1]
+    half = first.shape[0] // 2
     both = product(split(jnp.concatenate([first, second], 1)), table_z)
-    both = product(table_t, split(both))
+    even = product([table[:half] for table in table_t], split(both[:half] + both[half:]))
+    odd = product([table[half:] for table in table_t], split(both[:half] - both[half:]))
+    both = jnp.concatenate([even + odd, even - odd], 0)
     return both[:, :count_z], both[:, count_z:]
 
 
@@ -104,7 +113,7 @@
     radii, count_t, count_z = field.shape
     plane = pl.BlockSpec((2, count_t, count_z), lambda p: (p, 0, 0))
     packed = pl.BlockSpec((parts, 24, count_z), lambda p: (0, p, 0))
-    whole_t = pl.BlockSpec((count_t, count_t), lambda p: (0, 0))
+    whole_t = pl.BlockSpec((count_t, count_t // 2), lambda p: (0, 0))
     whole_z = pl.BlockSpec((2 * count_z, 2 * count_z), lambda p: (0, 0))
     shape = jax.ShapeDtypeStruct((parts, 12 * radii, count_z), jnp.float32)
     return pl.pallas_call(
@@ -160,6 +169,29 @@
         out_specs=vmem,
         name="coefficient_stage",
     )(base)
+
+
+def mix_body(mix_ref, order_ref, high_ref, low_ref):
+    order = order_ref[...]
+    for part, out_ref in zip(split(mix_ref[...]), (high_ref, low_ref)):
+        part = lax.dot_general(order, part, (((1,), (0,)), ((), ())), preferred_element_type=jnp.float32)
+        part = part.astype(jnp.bfloat16)
+        part = lax.dot_general(part, order, (((1,), (1,)), ((), ())), preferred_element_type=jnp.float32)
+        out_ref[...] = part.astype(jnp.bfloat16)
+
+
+def mix_stage(mix, parts):
+    size = mix.shape[0]
+    order = np.eye(size)[np.arange(size).reshape(parts, -1).T.reshape(-1)].astype(ml_dtypes.bfloat16)
+    vmem = pl.BlockSpec(memory_space=pltpu.VMEM)
+    shape = pltpu.VMEM(mix.shape, jnp.bfloat16)
+    return pl.pallas_call(
+        mix_body,
+        out_shape=(shape, shape),
+        in_specs=[vmem] * 2,
+        out_specs=(vmem, vmem),
+        name="mix_stage",
+    )(mix, order)
 
 
 def radial_body(state_ref, scale_ref, high_ref, low_ref, out_ref):
@@ -252,9 +284,11 @@
 
     late = (STAGGER * ((segment + 1) // 2 % 2)).astype(jnp.int32)[None]
     with jax.named_scope("first_filter"):
-        pair_z = np.kron(np.eye(2, dtype=np.float32), table_z)
+        pair_z = np.kron(np.eye(2), table_z)
+        rows = np.arange(count_t // 2)
+        half_t = split_constant(halves(table_t)[np.concatenate([rows, count_t + rows])])
         filtered, base_packed = first_stage(
-            state, base[0], split_constant(table_t), split_constant(pair_z), parts
+            state, base[0], half_t, split_constant(pair_z), parts
         )
     with jax.named_scope("shift_state"):
         filtered = from_behind(filtered, "seg", 1)
@@ -267,8 +301,7 @@
     with jax.named_scope("state_to_points"):
         points = swap(filtered)
     with jax.named_scope("radial"):
-        mix = radial_step.reshape(parts, 6, parts, 6).transpose(1, 0, 3, 2).reshape(radial_step.shape)
-        points = radial_stage(points.reshape(-1, count_z), scale, split_array(mix))
+        points = radial_stage(points.reshape(-1, count_z), scale, mix_stage(radial_step, parts))
     with jax.named_scope("state_to_radii"):
         carried = swap(points.reshape(parts, -1, count_z))
 
@@ -276,10 +309,12 @@
         closing = segment == first_segment[0] % lax.axis_size("seg")
         places_t = jnp.arange(count_t, dtype=jnp.int32)
         places_z = jnp.arange(count_z, dtype=jnp.int32)
+        places_t = places_t[: count_t // 2]
         index_t = jnp.where(closing, (az_shift[0] - places_t) % count_t, places_t)
+        index_t = jnp.concatenate([index_t, count_t + index_t])
         index_z = jnp.where(closing, (places_z + ax_shift[0]) % count_z, places_z)
-        last_t = split_array(jnp.take(jnp.asarray(table_t), index_t, axis=0))
-        last_z = jnp.take(jnp.asarray(table_z), index_z, axis=0).T
+        last_t = split_array(jnp.take(jnp.asarray(halves(table_t).astype(np.float32)), index_t, axis=0))
+        last_z = jnp.take(jnp.asarray(table_z.astype(np.float32)), index_z, axis=0).T
         last_z = split_array(jnp.kron(jnp.eye(2, dtype=jnp.float32), last_z))
     with jax.named_scope("last_filter"):
         return last_stage(carried.reshape(-1, count_z), state, last_t, last_z)[None]

time: 196 us -> 193 us (0.985)
  local copies, waits for them, and re-layouts: 11.4 us -> 3.42 us
  starting transfers between devices: 53.3 us -> 60.5 us
  waiting for transfers between devices: 112 us -> 109 us
    all_to_all x3, waiting for transfers between devices: 103 us -> 93.2 us  [swap(): return lax.all_to_all(packed, 'space', 0, 0, tiled=True)]
    ppermute x2, waiting for transfers between devices: 8.76 us -> 15.8 us  [from_behind(): return lax.ppermute(block, axis, route)]
    reshape x2 -> x0, local copies, waits for them, and re-layouts: 5.18 us -> none  [shards(): radial_step.reshape(parts, 6, parts, 6).transpose(1, 0, 3, 2)]
    all_to_all x3, starting transfers between devices: 44.8 us -> 48.8 us  [swap(): return lax.all_to_all(packed, 'space', 0, 0, tiled=True)]
    ppermute x2, starting transfers between devices: 8.5 us -> 11.7 us  [from_behind(): return lax.ppermute(block, axis, route)]
    transpose x1 -> x0, local copies, waits for them, and re-layouts: 2.72 us -> none  [shards(): radial_step.reshape(parts, 6, parts, 6).transpose(1, 0, 3, 2)]
  transfers between devices with their start and end apart: 5 -> 5, of which waited for: 4 -> 4; matrix products, arithmetic and copies ran while one was open for 6% -> 2% of each run, Pallas kernels for 1% -> 2%
where the time goes in v5:
time: 193 us; the launch traced here: 192 us
  waiting for transfers between devices  109 us (56%)
  starting transfers between devices  60.5 us (31%)
  Pallas kernels  16 us (8%)
  local copies, waits for them, and re-layouts  3.42 us (2%)
  between operations  2.14 us (1%)
    all_to_all x3, waiting for transfers between devices, swap(): return lax.all_to_all(packed, 'space', 0, 0, tiled=True)  93.2 us
    all_to_all x3, starting transfers between devices, swap(): return lax.all_to_all(packed, 'space', 0, 0, tiled=True)  48.8 us
    ppermute x2, waiting for transfers between devices, from_behind(): return lax.ppermute(block, axis, route)  15.8 us
    ppermute x2, starting transfers between devices, from_behind(): return lax.ppermute(block, axis, route)  11.7 us
    pallas_call x1, Pallas kernels, first_stage(): pl.pallas_call(first_body, out_shape=(shape, shape), grid=(radii // 2,),...  5.45 us
    pallas_call x1, Pallas kernels, last_stage(): pl.pallas_call(last_body, out_shape=jax.ShapeDtypeStruct(field.shape, jnp...  4.28 us
  transfers between devices with their start and end apart: 5, of which 4 were waited for; matrix products, arithmetic and copies ran while one was open for 2% of the time, Pallas kernels for 2%

profile of v5, /device:TPU:1, one launch (start us, length us, event | category | flops | bytes accessed | tf_op | source)
XLA Modules:
  0.0 191.7 jit_solution(11073739266593775924)
XLA Ops:
  0.0 5.4 %first_stage.1 = (f32[32,72,128]{2,1,0:T(8,128)}, f32[32,72,128]{2,1,0:T(8,128)}) custom-call(f32[6,384,128]{2,1,0:T(8,128)} %bitcast.31, f32[6,384,128]{2,1,0:T(8,128)} %bitcast.33, bf16[384,192]{1,0:T(8,128)(2,1)} %constant.114.clone.th_ref, bf16[384,192]{1,0:T(8,128)(2,1)} %constant.115.clone.tl_ref, bf16[256,256]{1,0:T(8,128)(2,1)} %constant.116.clone.zh_ref, ...), custom_call_target="tpu_custom_call" | custom-call | tf_op jit(solution)/shard_map/first_filter/first_stage/pallas_call | solution.py:119
  5.4 6.0 %collective-permute-start = (f32[32,72,128]{2,1,0:T(8,128)}, f32[32,72,128]{2,1,0:T(8,128)S(1)}, u32[]{:S(2)}, u32[]{:S(2)}) collective-permute-start(f32[32,72,128]{2,1,0:T(8,128)} %get-tuple-element.9), channel_id=1, source_target_pairs={{480,0},{0,32},{32,64},{64,96},{96,128},{128,160},{160,192},{192,2... | collective-permute-start | bytes 3538952 | tf_op jit(solution)/shard_map/shift_state/ppermute | solution.py:62
  11.5 37.3 %all-to-all-start.1 = ((f32[32,72,128]{2,1,0:T(8,128)}), f32[32,72,128]{2,1,0:T(8,128)}, u32[]{:S(2)}, u32[]{:S(2)}) async-start(f32[32,72,128]{2,1,0:T(8,128)} %hold.3), calls=%async_computation.1 | async-start | bytes 2359296 | tf_op jit(solution)/shard_map/base_to_points/all_to_all | solution.py:274
  48.9 0.0 collective-permute-done.block_ref
  48.9 0.0 copy-start.2
  48.9 1.0 copy-done.2
  49.9 40.4 %all-to-all-done.1 = f32[32,72,128]{2,1,0:T(8,128)} async-done(((f32[32,72,128]{2,1,0:T(8,128)}), f32[32,72,128]{2,1,0:T(8,128)}, u32[]{:S(2)}, u32[]{:S(2)}) %all-to-all-start.1) | async-done | bytes 1179680 | tf_op jit(solution)/shard_map/base_to_points/all_to_all | solution.py:274
  90.3 7.4 %all-to-all-start = ((f32[32,72,128]{2,1,0:T(8,128)}), f32[32,72,128]{2,1,0:T(8,128)S(1)}, u32[]{:S(2)}, u32[]{:S(2)}) async-start(f32[32,72,128]{2,1,0:T(8,128)} %hold.2), calls=%async_computation | async-start | bytes 2359296 | tf_op jit(solution)/shard_map/state_to_points/all_to_all | solution.py:274
  97.7 2.5 %coefficient_stage.1 = f32[12,192,128]{2,1,0:T(8,128)} custom-call(f32[2304,128]{1,0:T(8,128)} %bitcast.4.base_ref), custom_call_target="tpu_custom_call" | custom-call | tf_op jit(solution)/shard_map/shift_base/coefficient_stage/pallas_call | solution.py:165
  100.3 5.6 %collective-permute-start.1 = (f32[12,192,128]{2,1,0:T(8,128)}, f32[12,192,128]{2,1,0:T(8,128)S(1)}, u32[]{:S(2)}, u32[]{:S(2)}) collective-permute-start(f32[12,192,128]{2,1,0:T(8,128)} %coefficient_stage.1), channel_id=1, source_target_pairs={{480,0},{0,32},{32,64},{64,96},{96,128},{128,160},{160,192},{192,2... | collective-permute-start | bytes 3538952 | tf_op jit(solution)/shard_map/shift_base/ppermute | solution.py:62
  105.9 1.3 mix_stage.1
  107.2 15.8 %collective-permute-done.1.scale_ref = f32[12,192,128]{2,1,0:T(8,128)S(1)} collective-permute-done((f32[12,192,128]{2,1,0:T(8,128)}, f32[12,192,128]{2,1,0:T(8,128)S(1)}, u32[]{:S(2)}, u32[]{:S(2)}) %collective-permute-start.1) | collective-permute-done | bytes 1179680 | tf_op jit(solution)/shard_map/shift_base/ppermute | solution.py:62
  123.1 14.5 %all-to-all-done = f32[32,72,128]{2,1,0:T(8,128)S(1)} async-done(((f32[32,72,128]{2,1,0:T(8,128)}), f32[32,72,128]{2,1,0:T(8,128)S(1)}, u32[]{:S(2)}, u32[]{:S(2)}) %all-to-all-start) | async-done | bytes 1179680 | tf_op jit(solution)/shard_map/state_to_points/all_to_all | solution.py:274
  137.5 2.4 %radial_stage.1 = f32[2304,128]{1,0:T(8,128)} custom-call(f32[2304,128]{1,0:T(8,128)S(1)} %bitcast.28, f32[12,192,128]{2,1,0:T(8,128)S(1)} %collective-permute-done.1.scale_ref, bf16[192,192]{1,0:T(8,128)(2,1)S(1)} %get-tuple-element.11.high_ref, bf16[192,192]{1,0:T(8,128)(2,1)S(1)} %get-tuple-element.12.low_ref), custom_call_target="tpu_custom_call" | custom-call | tf_op jit(solution)/shard_map/radial/radial_stage/pallas_call | solution.py:218
  139.9 0.0 copy-start.1
  139.9 0.0 copy-start
  139.9 4.1 %all-to-all-start.2 = ((f32[32,72,128]{2,1,0:T(8,128)}), f32[32,72,128]{2,1,0:T(8,128)S(1)}, u32[]{:S(2)}, u32[]{:S(2)}) async-start(f32[32,72,128]{2,1,0:T(8,128)} %bitcast.30), calls=%async_computation.2 | async-start | bytes 2359296 | tf_op jit(solution)/shard_map/state_to_radii/all_to_all | solution.py:274
  146.0 0.0 copy-done.1
  146.0 0.6 gather_fusion.1
  146.7 0.1 select_bitcast_fusion
  146.8 0.1 copy.17
  146.9 0.1 fusion.2
  147.0 0.0 copy-done
  147.0 1.7 gather_fusion
  148.7 0.1 compare_and_fusion.1
  148.8 0.1 broadcast_multiply_fusion
  149.0 0.1 fusion
  149.1 38.3 %all-to-all-done.2 = f32[32,72,128]{2,1,0:T(8,128)S(1)} async-done(((f32[32,72,128]{2,1,0:T(8,128)}), f32[32,72,128]{2,1,0:T(8,128)S(1)}, u32[]{:S(2)}, u32[]{:S(2)}) %all-to-all-start.2) | async-done | bytes 1179680 | tf_op jit(solution)/shard_map/state_to_radii/all_to_all | solution.py:274
  187.4 4.3 %last_stage.1 = f32[6,384,128]{2,1,0:T(8,128)} custom-call(f32[2304,128]{1,0:T(8,128)S(1)} %bitcast.29, f32[6,384,128]{2,1,0:T(8,128)} %bitcast.32, bf16[384,192]{1,0:T(8,128)(2,1)S(1)} %get-tuple-element.16.th_ref, bf16[384,192]{1,0:T(8,128)(2,1)S(1)} %get-tuple-element.15.tl_ref, bf16[256,256]{1,0:T(8,128)(2,1)S(1)} %get-tuple-element.18.zh_ref, ...), custom_call_target="tpu_custom_call" | custom-call | tf_op jit(solution)/shard_map/last_filter/last_stage/pallas_call | solution.py:258
  (10 shorter events, 0.1 us)
Async XLA Ops:
  5.4 43.4 %collective-permute-start = (f32[32,72,128]{2,1,0:T(8,128)}, f32[32,72,128]{2,1,0:T(8,128)S(1)}, u32[]{:S(2)}, u32[]{:S(2)}) collective-permute-start(f32[32,72,128]{2,1,0:T(8,128)} %get-tuple-element.9), channel_id=1, source_target_pairs={{480,0},{0,32},{32,64},{64,96},{96,128},{128,160},{160,192},{192,2... | collective-permute-start | bytes 3538952 | tf_op jit(solution)/shard_map/shift_state/ppermute | solution.py:62
  11.5 78.7 %all-to-all-start.1 = ((f32[32,72,128]{2,1,0:T(8,128)}), f32[32,72,128]{2,1,0:T(8,128)}, u32[]{:S(2)}, u32[]{:S(2)}) async-start(f32[32,72,128]{2,1,0:T(8,128)} %hold.3), calls=%async_computation.1 | async-start | bytes 2359296 | tf_op jit(solution)/shard_map/base_to_points/all_to_all | solution.py:274
  48.9 1.0 copy-start.2
  90.3 47.3 %all-to-all-start = ((f32[32,72,128]{2,1,0:T(8,128)}), f32[32,72,128]{2,1,0:T(8,128)S(1)}, u32[]{:S(2)}, u32[]{:S(2)}) async-start(f32[32,72,128]{2,1,0:T(8,128)} %hold.2), calls=%async_computation | async-start | bytes 2359296 | tf_op jit(solution)/shard_map/state_to_points/all_to_all | solution.py:274
  100.3 22.8 %collective-permute-start.1 = (f32[12,192,128]{2,1,0:T(8,128)}, f32[12,192,128]{2,1,0:T(8,128)S(1)}, u32[]{:S(2)}, u32[]{:S(2)}) collective-permute-start(f32[12,192,128]{2,1,0:T(8,128)} %coefficient_stage.1), channel_id=1, source_target_pairs={{480,0},{0,32},{32,64},{64,96},{96,128},{128,160},{160,192},{192,2... | collective-permute-start | bytes 3538952 | tf_op jit(solution)/shard_map/shift_base/ppermute | solution.py:62
  139.9 6.1 %copy-start.1 = (f32[128,128]{1,0:T(8,128)S(1)}, f32[128,128]{1,0:T(8,128)}, u32[]{:S(2)}) copy-start(f32[128,128]{1,0:T(8,128)} %constant.120.clone) | copy-start | bytes 196612
  139.9 7.1 %copy-start = (f32[768,192]{1,0:T(8,128)S(1)}, f32[768,192]{1,0:T(8,128)}, u32[]{:S(2)}) copy-start(f32[768,192]{1,0:T(8,128)} %constant.119.clone) | copy-start | bytes 1769476
  139.9 47.5 %all-to-all-start.2 = ((f32[32,72,128]{2,1,0:T(8,128)}), f32[32,72,128]{2,1,0:T(8,128)S(1)}, u32[]{:S(2)}, u32[]{:S(2)}) async-start(f32[32,72,128]{2,1,0:T(8,128)} %bitcast.30), calls=%async_computation.2 | async-start | bytes 2359296 | tf_op jit(solution)/shard_map/state_to_radii/all_to_all | solution.py:274

commit v6 on v5

--- a/solution.py
+++ b/solution.py
@@ -11,7 +11,7 @@
 
 STEP_SIZE = 0.25
 VISCOUS_RATE = 1.5e-05
-STAGGER = 22000
+STAGGER = 25000
 TILE = 8
 
 
@@ -101,8 +101,30 @@
     return both[:, :count_z], both[:, count_z:]
 
 
-def first_body(field_ref, base_ref, th_ref, tl_ref, zh_ref, zl_ref, state_ref, base_out_ref):
-    pack_pair(base_out_ref, base_ref[0], base_ref[1])
+def pack_body(late_ref, base_ref, out_ref):
+    pack_pair(out_ref, base_ref[0], base_ref[1])
+
+    @pl.when(pl.program_id(0) == pl.num_programs(0) - 1)
+    def _():
+        pl.delay(late_ref[0])
+
+
+def pack_stage(base, parts, late):
+    radii, count_t, count_z = base.shape
+    return pl.pallas_call(
+        pack_body,
+        out_shape=jax.ShapeDtypeStruct((parts, 12 * radii, count_z), jnp.float32),
+        grid=(radii // 2,),
+        in_specs=[
+            pl.BlockSpec(memory_space=pltpu.SMEM),
+            pl.BlockSpec((2, count_t, count_z), lambda p: (p, 0, 0)),
+        ],
+        out_specs=pl.BlockSpec((parts, 24, count_z), lambda p: (0, p, 0)),
+        name="pack_stage",
+    )(late, base)
+
+
+def first_body(field_ref, base_ref, th_ref, tl_ref, zh_ref, zl_ref, state_ref):
     forced = [field_ref[k] + STEP_SIZE * base_ref[k] * field_ref[k] for k in range(2)]
     table_t = (th_ref[...], tl_ref[...])
     table_z = (zh_ref[...], zl_ref[...])
@@ -112,35 +134,16 @@
 def first_stage(field, base, table_t, table_z, parts):
     radii, count_t, count_z = field.shape
     plane = pl.BlockSpec((2, count_t, count_z), lambda p: (p, 0, 0))
-    packed = pl.BlockSpec((parts, 24, count_z), lambda p: (0, p, 0))
     whole_t = pl.BlockSpec((count_t, count_t // 2), lambda p: (0, 0))
     whole_z = pl.BlockSpec((2 * count_z, 2 * count_z), lambda p: (0, 0))
-    shape = jax.ShapeDtypeStruct((parts, 12 * radii, count_z), jnp.float32)
     return pl.pallas_call(
         first_body,
-        out_shape=(shape, shape),
+        out_shape=jax.ShapeDtypeStruct((parts, 12 * radii, count_z), jnp.float32),
         grid=(radii // 2,),
         in_specs=[plane, plane, whole_t, whole_t, whole_z, whole_z],
-        out_specs=(packed, packed),
+        out_specs=pl.BlockSpec((parts, 24, count_z), lambda p: (0, p, 0)),
         name="first_stage",
     )(field, base, *table_t, *table_z)
-
-
-def hold_body(late_ref, block_ref, out_ref):
-    pl.delay(late_ref[0])
-
-
-def hold(block, late, weight):
-    whole = pl.BlockSpec(memory_space=pl.ANY)
-    return pl.pallas_call(
-        hold_body,
-        out_shape=jax.ShapeDtypeStruct(block.shape, block.dtype),
-        in_specs=[pl.BlockSpec(memory_space=pltpu.SMEM), whole],
-        out_specs=whole,
-        input_output_aliases={1: 0},
-        cost_estimate=pl.CostEstimate(flops=weight * 1000, transcendentals=0, bytes_accessed=0),
-        name="hold",
-    )(late, block)
 
 
 def row_of(pair, half, point):
@@ -283,18 +286,17 @@
     table_z = filter_table(count_z)
 
     late = (STAGGER * ((segment + 1) // 2 % 2)).astype(jnp.int32)[None]
+    with jax.named_scope("pack_base"):
+        base_packed = pack_stage(base[0], parts, late)
+    with jax.named_scope("base_to_points"):
+        base_points = swap(base_packed)
     with jax.named_scope("first_filter"):
         pair_z = np.kron(np.eye(2), table_z)
         rows = np.arange(count_t // 2)
         half_t = split_constant(halves(table_t)[np.concatenate([rows, count_t + rows])])
-        filtered, base_packed = first_stage(
-            state, base[0], half_t, split_constant(pair_z), parts
-        )
+        filtered = first_stage(state, base[0], half_t, split_constant(pair_z), parts)
     with jax.named_scope("shift_state"):
         filtered = from_behind(filtered, "seg", 1)
-        filtered = hold(filtered, jnp.zeros_like(late), 1 << 30)
-    with jax.named_scope("base_to_points"):
-        base_points = swap(hold(base_packed, late, 0))
     with jax.named_scope("shift_base"):
         scale = coefficient_stage(base_points.reshape(-1, count_z), parts)
         scale = from_behind(scale, "seg", 1)

time: 193 us -> 189 us (0.979)
  Pallas kernels: 16 us -> 43.8 us
  starting transfers between devices: 60.5 us -> 39.1 us
  waiting for transfers between devices: 109 us -> 100 us
    pallas_call x3 -> x2, Pallas kernels: 5.45 us -> 33.3 us  [the longest x1 28.2 us: pack_stage(): pl.pallas_call(pack_body, out_shape=jax.ShapeDtypeStruct((parts, 12 * rad...]
    all_to_all x3, waiting for transfers between devices: 93.2 us -> 66.4 us  [swap(): return lax.all_to_all(packed, 'space', 0, 0, tiled=True)]
    all_to_all x3, starting transfers between devices: 48.8 us -> 28.2 us  [swap(): return lax.all_to_all(packed, 'space', 0, 0, tiled=True)]
    ppermute x2, waiting for transfers between devices: 15.8 us -> 33.8 us  [from_behind(): return lax.ppermute(block, axis, route)]
  transfers between devices with their start and end apart: 5 -> 5, of which waited for: 4 -> 5; matrix products, arithmetic and copies ran while one was open for 2% -> 2% of each run, Pallas kernels for 2% -> 5%
where the time goes in v6:
time: 189 us; the launch traced here: 188 us
  waiting for transfers between devices  100 us (53%)
  Pallas kernels  43.8 us (23%)
  starting transfers between devices  39.1 us (21%)
  local copies, waits for them, and re-layouts  2.42 us (1%)
  between operations  2.1 us (1%)
    all_to_all x3, waiting for transfers between devices, swap(): return lax.all_to_all(packed, 'space', 0, 0, tiled=True)  66.4 us
    ppermute x2, waiting for transfers between devices, from_behind(): return lax.ppermute(block, axis, route)  33.8 us
    all_to_all x3, starting transfers between devices, swap(): return lax.all_to_all(packed, 'space', 0, 0, tiled=True)  28.2 us
    pallas_call x1, Pallas kernels, pack_stage(): pl.pallas_call(pack_body, out_shape=jax.ShapeDtypeStruct((parts, 12 * rad...  28.2 us
    ppermute x2, starting transfers between devices, from_behind(): return lax.ppermute(block, axis, route)  10.8 us
    pallas_call x1, Pallas kernels, first_stage(): pl.pallas_call(first_body, out_shape=jax.ShapeDtypeStruct((parts, 12 * ra...  5.11 us
    pallas_call x1, Pallas kernels, last_stage(): pl.pallas_call(last_body, out_shape=jax.ShapeDtypeStruct(field.shape, jnp...  4.28 us
  transfers between devices with their start and end apart: 5, of which 5 were waited for; matrix products, arithmetic and copies ran while one was open for 2% of the time, Pallas kernels for 5%

profile of v6, /device:TPU:1, one launch (start us, length us, event | category | flops | bytes accessed | tf_op | source)
XLA Modules:
  0.0 188.2 jit_solution(442280530251454997)
XLA Ops:
  0.0 28.2 %pack_stage.1 = f32[32,72,128]{2,1,0:T(8,128)} custom-call(s32[1]{0:T(128)} %bitcast.3.late_ref, f32[6,384,128]{2,1,0:T(8,128)} %bitcast.32), custom_call_target="tpu_custom_call" | custom-call | tf_op jit(solution)/shard_map/pack_base/pack_stage/pallas_call | solution.py:114
  28.2 17.0 %all-to-all-start.1 = ((f32[32,72,128]{2,1,0:T(8,128)}), f32[32,72,128]{2,1,0:T(8,128)S(1)}, u32[]{:S(2)}, u32[]{:S(2)}) async-start(f32[32,72,128]{2,1,0:T(8,128)} %pack_stage.1), calls=%async_computation.1 | async-start | bytes 2359296 | tf_op jit(solution)/shard_map/base_to_points/all_to_all | solution.py:277
  45.1 5.1 %first_stage.1 = f32[32,72,128]{2,1,0:T(8,128)} custom-call(f32[6,384,128]{2,1,0:T(8,128)} %bitcast.34, f32[6,384,128]{2,1,0:T(8,128)} %bitcast.33, bf16[384,192]{1,0:T(8,128)(2,1)} %constant.112.clone.th_ref, bf16[384,192]{1,0:T(8,128)(2,1)} %constant.113.clone.tl_ref, bf16[256,256]{1,0:T(8,128)(2,1)} %constant.114.clone.zh_ref, ...), custom_call_target="tpu_custom_call" | custom-call | tf_op jit(solution)/shard_map/first_filter/first_stage/pallas_call | solution.py:139
  50.2 5.2 %collective-permute-start = (f32[32,72,128]{2,1,0:T(8,128)}, f32[32,72,128]{2,1,0:T(8,128)}, u32[]{:S(2)}, u32[]{:S(2)}) collective-permute-start(f32[32,72,128]{2,1,0:T(8,128)} %first_stage.1), channel_id=1, source_target_pairs={{480,0},{0,32},{32,64},{64,96},{96,128},{128,160},{160,192},{192,2... | collective-permute-start | bytes 3538952 | tf_op jit(solution)/shard_map/shift_state/ppermute | solution.py:62
  55.4 17.7 %collective-permute-done = f32[32,72,128]{2,1,0:T(8,128)} collective-permute-done((f32[32,72,128]{2,1,0:T(8,128)}, f32[32,72,128]{2,1,0:T(8,128)}, u32[]{:S(2)}, u32[]{:S(2)}) %collective-permute-start) | collective-permute-done | bytes 1179680 | tf_op jit(solution)/shard_map/shift_state/ppermute | solution.py:62
  73.2 13.2 %all-to-all-done.1 = f32[32,72,128]{2,1,0:T(8,128)S(1)} async-done(((f32[32,72,128]{2,1,0:T(8,128)}), f32[32,72,128]{2,1,0:T(8,128)S(1)}, u32[]{:S(2)}, u32[]{:S(2)}) %all-to-all-start.1) | async-done | bytes 1179680 | tf_op jit(solution)/shard_map/base_to_points/all_to_all | solution.py:277
  86.4 0.0 copy-start.1
  86.4 7.2 %all-to-all-start = ((f32[32,72,128]{2,1,0:T(8,128)}), f32[32,72,128]{2,1,0:T(8,128)S(1)}, u32[]{:S(2)}, u32[]{:S(2)}) async-start(f32[32,72,128]{2,1,0:T(8,128)} %collective-permute-done), calls=%async_computation | async-start | bytes 2359296 | tf_op jit(solution)/shard_map/state_to_points/all_to_all | solution.py:277
  93.6 0.0 copy-done.1
  93.6 2.5 %coefficient_stage.1 = f32[12,192,128]{2,1,0:T(8,128)} custom-call(f32[2304,128]{1,0:T(8,128)} %bitcast.31), custom_call_target="tpu_custom_call" | custom-call | tf_op jit(solution)/shard_map/shift_base/coefficient_stage/pallas_call | solution.py:168
  96.1 5.6 %collective-permute-start.1 = (f32[12,192,128]{2,1,0:T(8,128)}, f32[12,192,128]{2,1,0:T(8,128)S(1)}, u32[]{:S(2)}, u32[]{:S(2)}) collective-permute-start(f32[12,192,128]{2,1,0:T(8,128)} %coefficient_stage.1), channel_id=1, source_target_pairs={{480,0},{0,32},{32,64},{64,96},{96,128},{128,160},{160,192},{192,2... | collective-permute-start | bytes 3538952 | tf_op jit(solution)/shard_map/shift_base/ppermute | solution.py:62
  101.8 1.3 mix_stage.1
  103.2 16.1 %collective-permute-done.1.scale_ref = f32[12,192,128]{2,1,0:T(8,128)S(1)} collective-permute-done((f32[12,192,128]{2,1,0:T(8,128)}, f32[12,192,128]{2,1,0:T(8,128)S(1)}, u32[]{:S(2)}, u32[]{:S(2)}) %collective-permute-start.1) | collective-permute-done | bytes 1179680 | tf_op jit(solution)/shard_map/shift_base/ppermute | solution.py:62
  119.3 14.1 %all-to-all-done = f32[32,72,128]{2,1,0:T(8,128)S(1)} async-done(((f32[32,72,128]{2,1,0:T(8,128)}), f32[32,72,128]{2,1,0:T(8,128)S(1)}, u32[]{:S(2)}, u32[]{:S(2)}) %all-to-all-start) | async-done | bytes 1179680 | tf_op jit(solution)/shard_map/state_to_points/all_to_all | solution.py:277
  133.4 2.4 %radial_stage.1 = f32[2304,128]{1,0:T(8,128)} custom-call(f32[2304,128]{1,0:T(8,128)S(1)} %bitcast.28, f32[12,192,128]{2,1,0:T(8,128)S(1)} %collective-permute-done.1.scale_ref, bf16[192,192]{1,0:T(8,128)(2,1)S(1)} %get-tuple-element.7.high_ref, bf16[192,192]{1,0:T(8,128)(2,1)S(1)} %get-tuple-element.8.low_ref), custom_call_target="tpu_custom_call" | custom-call | tf_op jit(solution)/shard_map/radial/radial_stage/pallas_call | solution.py:221
  135.8 0.0 copy-start.2
  135.8 0.0 copy-start
  135.8 4.1 %all-to-all-start.2 = ((f32[32,72,128]{2,1,0:T(8,128)}), f32[32,72,128]{2,1,0:T(8,128)S(1)}, u32[]{:S(2)}, u32[]{:S(2)}) async-start(f32[32,72,128]{2,1,0:T(8,128)} %bitcast.30), calls=%async_computation.2 | async-start | bytes 2359296 | tf_op jit(solution)/shard_map/state_to_radii/all_to_all | solution.py:277
  141.8 0.0 copy-done.2
  141.9 0.6 gather_fusion.1
  142.5 0.1 select_bitcast_fusion
  142.6 0.1 copy.15
  142.7 0.1 fusion.2
  142.8 0.0 copy-done
  142.8 1.7 gather_fusion
  144.5 0.1 compare_and_fusion.1
  144.6 0.1 broadcast_multiply_fusion
  144.8 0.1 fusion
  144.9 39.0 %all-to-all-done.2 = f32[32,72,128]{2,1,0:T(8,128)S(1)} async-done(((f32[32,72,128]{2,1,0:T(8,128)}), f32[32,72,128]{2,1,0:T(8,128)S(1)}, u32[]{:S(2)}, u32[]{:S(2)}) %all-to-all-start.2) | async-done | bytes 1179680 | tf_op jit(solution)/shard_map/state_to_radii/all_to_all | solution.py:277
  184.0 4.3 %last_stage.1 = f32[6,384,128]{2,1,0:T(8,128)} custom-call(f32[2304,128]{1,0:T(8,128)S(1)} %bitcast.29, f32[6,384,128]{2,1,0:T(8,128)} %bitcast.35, bf16[384,192]{1,0:T(8,128)(2,1)S(1)} %get-tuple-element.12.th_ref, bf16[384,192]{1,0:T(8,128)(2,1)S(1)} %get-tuple-element.11.tl_ref, bf16[256,256]{1,0:T(8,128)(2,1)S(1)} %get-tuple-element.14.zh_ref, ...), custom_call_target="tpu_custom_call" | custom-call | tf_op jit(solution)/shard_map/last_filter/last_stage/pallas_call | solution.py:261
  (8 shorter events, 0.1 us)
Async XLA Ops:
  28.2 58.2 %all-to-all-start.1 = ((f32[32,72,128]{2,1,0:T(8,128)}), f32[32,72,128]{2,1,0:T(8,128)S(1)}, u32[]{:S(2)}, u32[]{:S(2)}) async-start(f32[32,72,128]{2,1,0:T(8,128)} %pack_stage.1), calls=%async_computation.1 | async-start | bytes 2359296 | tf_op jit(solution)/shard_map/base_to_points/all_to_all | solution.py:277
  50.2 22.9 %collective-permute-start = (f32[32,72,128]{2,1,0:T(8,128)}, f32[32,72,128]{2,1,0:T(8,128)}, u32[]{:S(2)}, u32[]{:S(2)}) collective-permute-start(f32[32,72,128]{2,1,0:T(8,128)} %first_stage.1), channel_id=1, source_target_pairs={{480,0},{0,32},{32,64},{64,96},{96,128},{128,160},{160,192},{192,2... | collective-permute-start | bytes 3538952 | tf_op jit(solution)/shard_map/shift_state/ppermute | solution.py:62
  86.4 7.2 %copy-start.1 = (f32[32,72,128]{2,1,0:T(8,128)}, f32[32,72,128]{2,1,0:T(8,128)S(1)}, u32[]{:S(2)}) copy-start(f32[32,72,128]{2,1,0:T(8,128)S(1)} %all-to-all-done.1) | copy-start | bytes 3538948
  86.4 47.0 %all-to-all-start = ((f32[32,72,128]{2,1,0:T(8,128)}), f32[32,72,128]{2,1,0:T(8,128)S(1)}, u32[]{:S(2)}, u32[]{:S(2)}) async-start(f32[32,72,128]{2,1,0:T(8,128)} %collective-permute-done), calls=%async_computation | async-start | bytes 2359296 | tf_op jit(solution)/shard_map/state_to_points/all_to_all | solution.py:277
  96.1 23.1 %collective-permute-start.1 = (f32[12,192,128]{2,1,0:T(8,128)}, f32[12,192,128]{2,1,0:T(8,128)S(1)}, u32[]{:S(2)}, u32[]{:S(2)}) collective-permute-start(f32[12,192,128]{2,1,0:T(8,128)} %coefficient_stage.1), channel_id=1, source_target_pairs={{480,0},{0,32},{32,64},{64,96},{96,128},{128,160},{160,192},{192,2... | collective-permute-start | bytes 3538952 | tf_op jit(solution)/shard_map/shift_base/ppermute | solution.py:62
  135.8 6.1 %copy-start.2 = (f32[128,128]{1,0:T(8,128)S(1)}, f32[128,128]{1,0:T(8,128)}, u32[]{:S(2)}) copy-start(f32[128,128]{1,0:T(8,128)} %constant.118.clone) | copy-start | bytes 196612
  135.8 7.1 %copy-start = (f32[768,192]{1,0:T(8,128)S(1)}, f32[768,192]{1,0:T(8,128)}, u32[]{:S(2)}) copy-start(f32[768,192]{1,0:T(8,128)} %constant.117.clone) | copy-start | bytes 1769476
  135.8 48.2 %all-to-all-start.2 = ((f32[32,72,128]{2,1,0:T(8,128)}), f32[32,72,128]{2,1,0:T(8,128)S(1)}, u32[]{:S(2)}, u32[]{:S(2)}) async-start(f32[32,72,128]{2,1,0:T(8,128)} %bitcast.30), calls=%async_computation.2 | async-start | bytes 2359296 | tf_op jit(solution)/shard_map/state_to_radii/all_to_all | solution.py:277

commit v7 on v6

--- a/solution.py
+++ b/solution.py
@@ -101,25 +101,38 @@
     return both[:, :count_z], both[:, count_z:]
 
 
-def pack_body(late_ref, base_ref, out_ref):
-    pack_pair(out_ref, base_ref[0], base_ref[1])
-
-    @pl.when(pl.program_id(0) == pl.num_programs(0) - 1)
-    def _():
-        pl.delay(late_ref[0])
+def pack_body(late_ref, base_ref, out_ref, start, packed, start_sems, sems):
+    loads, copies = [], []
+    for pair in range(start.shape[0] // 2):
+        planes = pl.ds(2 * pair, 2)
+        loads.append(pltpu.make_async_copy(base_ref.at[planes], start.at[planes], start_sems.at[pair]))
+        loads[-1].start()
+    for pair, load in enumerate(loads):
+        rows = pl.ds(24 * pair, 24)
+        load.wait()
+        pack_pair(packed.at[:, rows, :], start[2 * pair], start[2 * pair + 1])
+        copies.append(pltpu.make_async_copy(packed.at[:, rows, :], out_ref.at[:, rows, :], sems.at[pair]))
+        copies[-1].start()
+    pl.delay(late_ref[0])
+    for copy in copies:
+        copy.wait()
 
 
 def pack_stage(base, parts, late):
     radii, count_t, count_z = base.shape
+    shape = (parts, 12 * radii, count_z)
+    hbm = pl.BlockSpec(memory_space=pltpu.HBM)
     return pl.pallas_call(
         pack_body,
-        out_shape=jax.ShapeDtypeStruct((parts, 12 * radii, count_z), jnp.float32),
-        grid=(radii // 2,),
-        in_specs=[
-            pl.BlockSpec(memory_space=pltpu.SMEM),
-            pl.BlockSpec((2, count_t, count_z), lambda p: (p, 0, 0)),
+        out_shape=jax.ShapeDtypeStruct(shape, jnp.float32),
+        in_specs=[pl.BlockSpec(memory_space=pltpu.SMEM), hbm],
+        out_specs=hbm,
+        scratch_shapes=[
+            pltpu.VMEM(base.shape, jnp.float32),
+            pltpu.VMEM(shape, jnp.float32),
+            pltpu.SemaphoreType.DMA((radii // 2,)),
+            pltpu.SemaphoreType.DMA((radii // 2,)),
         ],
-        out_specs=pl.BlockSpec((parts, 24, count_z), lambda p: (0, p, 0)),
         name="pack_stage",
     )(late, base)
 

time: 189 us -> 188 us (level)
  waiting for transfers between devices: 100 us -> 104 us
  starting transfers between devices: 39.1 us -> 37.1 us
    all_to_all x3, waiting for transfers between devices: 66.4 us -> 71.2 us  [swap(): return lax.all_to_all(packed, 'space', 0, 0, tiled=True)]
where the time goes in v7:
time: 188 us
  waiting for transfers between devices  104 us (55%)
  Pallas kernels  42 us (22%)
  starting transfers between devices  37.1 us (20%)
  local copies, waits for them, and re-layouts  2.42 us (1%)
  between operations  2.11 us (1%)
    all_to_all x3, waiting for transfers between devices, swap(): return lax.all_to_all(packed, 'space', 0, 0, tiled=True)  71.2 us
    ppermute x2, waiting for transfers between devices, from_behind(): return lax.ppermute(block, axis, route)  32.5 us
    all_to_all x3, starting transfers between devices, swap(): return lax.all_to_all(packed, 'space', 0, 0, tiled=True)  27.2 us
    pallas_call x1, Pallas kernels, pack_stage(): pl.pallas_call(pack_body, out_shape=jax.ShapeDtypeStruct(shape, jnp.float...  26.3 us
    ppermute x2, starting transfers between devices, from_behind(): return lax.ppermute(block, axis, route)  9.85 us
    pallas_call x1, Pallas kernels, first_stage(): pl.pallas_call(first_body, out_shape=jax.ShapeDtypeStruct((parts, 12 * ra...  5.11 us
    pallas_call x1, Pallas kernels, last_stage(): pl.pallas_call(last_body, out_shape=jax.ShapeDtypeStruct(field.shape, jnp...  4.28 us
  transfers between devices with their start and end apart: 5, of which 5 were waited for; matrix products, arithmetic and copies ran while one was open for 2% of the time, Pallas kernels for 5%

profile of v7, /device:TPU:1, one launch (start us, length us, event | category | flops | bytes accessed | tf_op | source)
XLA Modules:
  0.0 187.9 jit_solution(16452868184102108571)
XLA Ops:
  0.0 26.3 %pack_stage.1 = f32[32,72,128]{2,1,0:T(8,128)} custom-call(s32[1]{0:T(128)} %bitcast.3.late_ref, f32[6,384,128]{2,1,0:T(8,128)} %bitcast.32), custom_call_target="tpu_custom_call" | custom-call | tf_op jit(solution)/shard_map/pack_base/pack_stage/pallas_call | solution.py:125
  26.3 17.0 %all-to-all-start.1 = ((f32[32,72,128]{2,1,0:T(8,128)}), f32[32,72,128]{2,1,0:T(8,128)S(1)}, u32[]{:S(2)}, u32[]{:S(2)}) async-start(f32[32,72,128]{2,1,0:T(8,128)} %pack_stage.1), calls=%async_computation.1 | async-start | bytes 2359296 | tf_op jit(solution)/shard_map/base_to_points/all_to_all | solution.py:290
  43.3 5.1 %first_stage.1 = f32[32,72,128]{2,1,0:T(8,128)} custom-call(f32[6,384,128]{2,1,0:T(8,128)} %bitcast.34, f32[6,384,128]{2,1,0:T(8,128)} %bitcast.33, bf16[384,192]{1,0:T(8,128)(2,1)} %constant.112.clone.th_ref, bf16[384,192]{1,0:T(8,128)(2,1)} %constant.113.clone.tl_ref, bf16[256,256]{1,0:T(8,128)(2,1)} %constant.114.clone.zh_ref, ...), custom_call_target="tpu_custom_call" | custom-call | tf_op jit(solution)/shard_map/first_filter/first_stage/pallas_call | solution.py:152
  48.4 5.2 %collective-permute-start = (f32[32,72,128]{2,1,0:T(8,128)}, f32[32,72,128]{2,1,0:T(8,128)}, u32[]{:S(2)}, u32[]{:S(2)}) collective-permute-start(f32[32,72,128]{2,1,0:T(8,128)} %first_stage.1), channel_id=1, source_target_pairs={{480,0},{0,32},{32,64},{64,96},{96,128},{128,160},{160,192},{192,2... | collective-permute-start | bytes 3538952 | tf_op jit(solution)/shard_map/shift_state/ppermute | solution.py:62
  53.6 17.4 %collective-permute-done = f32[32,72,128]{2,1,0:T(8,128)} collective-permute-done((f32[32,72,128]{2,1,0:T(8,128)}, f32[32,72,128]{2,1,0:T(8,128)}, u32[]{:S(2)}, u32[]{:S(2)}) %collective-permute-start) | collective-permute-done | bytes 1179680 | tf_op jit(solution)/shard_map/shift_state/ppermute | solution.py:62
  71.0 13.8 %all-to-all-done.1 = f32[32,72,128]{2,1,0:T(8,128)S(1)} async-done(((f32[32,72,128]{2,1,0:T(8,128)}), f32[32,72,128]{2,1,0:T(8,128)S(1)}, u32[]{:S(2)}, u32[]{:S(2)}) %all-to-all-start.1) | async-done | bytes 1179680 | tf_op jit(solution)/shard_map/base_to_points/all_to_all | solution.py:290
  84.9 0.0 copy-start.1
  84.9 6.2 %all-to-all-start = ((f32[32,72,128]{2,1,0:T(8,128)}), f32[32,72,128]{2,1,0:T(8,128)S(1)}, u32[]{:S(2)}, u32[]{:S(2)}) async-start(f32[32,72,128]{2,1,0:T(8,128)} %collective-permute-done), calls=%async_computation | async-start | bytes 2359296 | tf_op jit(solution)/shard_map/state_to_points/all_to_all | solution.py:290
  91.0 0.0 copy-done.1
  91.0 2.5 %coefficient_stage.1 = f32[12,192,128]{2,1,0:T(8,128)} custom-call(f32[2304,128]{1,0:T(8,128)} %bitcast.31), custom_call_target="tpu_custom_call" | custom-call | tf_op jit(solution)/shard_map/shift_base/coefficient_stage/pallas_call | solution.py:181
  93.6 4.7 %collective-permute-start.1 = (f32[12,192,128]{2,1,0:T(8,128)}, f32[12,192,128]{2,1,0:T(8,128)S(1)}, u32[]{:S(2)}, u32[]{:S(2)}) collective-permute-start(f32[12,192,128]{2,1,0:T(8,128)} %coefficient_stage.1), channel_id=1, source_target_pairs={{480,0},{0,32},{32,64},{64,96},{96,128},{128,160},{160,192},{192,2... | collective-permute-start | bytes 3538952 | tf_op jit(solution)/shard_map/shift_base/ppermute | solution.py:62
  98.3 1.3 mix_stage.1
  99.6 15.0 %collective-permute-done.1.scale_ref = f32[12,192,128]{2,1,0:T(8,128)S(1)} collective-permute-done((f32[12,192,128]{2,1,0:T(8,128)}, f32[12,192,128]{2,1,0:T(8,128)S(1)}, u32[]{:S(2)}, u32[]{:S(2)}) %collective-permute-start.1) | collective-permute-done | bytes 1179680 | tf_op jit(solution)/shard_map/shift_base/ppermute | solution.py:62
  114.6 17.8 %all-to-all-done = f32[32,72,128]{2,1,0:T(8,128)S(1)} async-done(((f32[32,72,128]{2,1,0:T(8,128)}), f32[32,72,128]{2,1,0:T(8,128)S(1)}, u32[]{:S(2)}, u32[]{:S(2)}) %all-to-all-start) | async-done | bytes 1179680 | tf_op jit(solution)/shard_map/state_to_points/all_to_all | solution.py:290
  132.5 2.4 %radial_stage.1 = f32[2304,128]{1,0:T(8,128)} custom-call(f32[2304,128]{1,0:T(8,128)S(1)} %bitcast.28, f32[12,192,128]{2,1,0:T(8,128)S(1)} %collective-permute-done.1.scale_ref, bf16[192,192]{1,0:T(8,128)(2,1)S(1)} %get-tuple-element.7.high_ref, bf16[192,192]{1,0:T(8,128)(2,1)S(1)} %get-tuple-element.8.low_ref), custom_call_target="tpu_custom_call" | custom-call | tf_op jit(solution)/shard_map/radial/radial_stage/pallas_call | solution.py:234
  134.9 0.0 copy-start.2
  134.9 0.0 copy-start
  134.9 4.1 %all-to-all-start.2 = ((f32[32,72,128]{2,1,0:T(8,128)}), f32[32,72,128]{2,1,0:T(8,128)S(1)}, u32[]{:S(2)}, u32[]{:S(2)}) async-start(f32[32,72,128]{2,1,0:T(8,128)} %bitcast.30), calls=%async_computation.2 | async-start | bytes 2359296 | tf_op jit(solution)/shard_map/state_to_radii/all_to_all | solution.py:290
  140.9 0.0 copy-done.2
  140.9 0.6 gather_fusion.1
  141.6 0.1 select_bitcast_fusion
  141.7 0.1 copy.15
  141.8 0.1 fusion.2
  141.9 0.0 copy-done
  141.9 1.7 gather_fusion
  143.6 0.1 compare_and_fusion.1
  143.7 0.1 broadcast_multiply_fusion
  143.9 0.1 fusion
  144.0 39.6 %all-to-all-done.2 = f32[32,72,128]{2,1,0:T(8,128)S(1)} async-done(((f32[32,72,128]{2,1,0:T(8,128)}), f32[32,72,128]{2,1,0:T(8,128)S(1)}, u32[]{:S(2)}, u32[]{:S(2)}) %all-to-all-start.2) | async-done | bytes 1179680 | tf_op jit(solution)/shard_map/state_to_radii/all_to_all | solution.py:290
  183.6 4.3 %last_stage.1 = f32[6,384,128]{2,1,0:T(8,128)} custom-call(f32[2304,128]{1,0:T(8,128)S(1)} %bitcast.29, f32[6,384,128]{2,1,0:T(8,128)} %bitcast.35, bf16[384,192]{1,0:T(8,128)(2,1)S(1)} %get-tuple-element.12.th_ref, bf16[384,192]{1,0:T(8,128)(2,1)S(1)} %get-tuple-element.11.tl_ref, bf16[256,256]{1,0:T(8,128)(2,1)S(1)} %get-tuple-element.14.zh_ref, ...), custom_call_target="tpu_custom_call" | custom-call | tf_op jit(solution)/shard_map/last_filter/last_stage/pallas_call | solution.py:274
  (8 shorter events, 0.1 us)
Async XLA Ops:
  26.3 58.5 %all-to-all-start.1 = ((f32[32,72,128]{2,1,0:T(8,128)}), f32[32,72,128]{2,1,0:T(8,128)S(1)}, u32[]{:S(2)}, u32[]{:S(2)}) async-start(f32[32,72,128]{2,1,0:T(8,128)} %pack_stage.1), calls=%async_computation.1 | async-start | bytes 2359296 | tf_op jit(solution)/shard_map/base_to_points/all_to_all | solution.py:290
  48.4 22.6 %collective-permute-start = (f32[32,72,128]{2,1,0:T(8,128)}, f32[32,72,128]{2,1,0:T(8,128)}, u32[]{:S(2)}, u32[]{:S(2)}) collective-permute-start(f32[32,72,128]{2,1,0:T(8,128)} %first_stage.1), channel_id=1, source_target_pairs={{480,0},{0,32},{32,64},{64,96},{96,128},{128,160},{160,192},{192,2... | collective-permute-start | bytes 3538952 | tf_op jit(solution)/shard_map/shift_state/ppermute | solution.py:62
  84.9 6.2 %copy-start.1 = (f32[32,72,128]{2,1,0:T(8,128)}, f32[32,72,128]{2,1,0:T(8,128)S(1)}, u32[]{:S(2)}) copy-start(f32[32,72,128]{2,1,0:T(8,128)S(1)} %all-to-all-done.1) | copy-start | bytes 3538948
  84.9 47.6 %all-to-all-start = ((f32[32,72,128]{2,1,0:T(8,128)}), f32[32,72,128]{2,1,0:T(8,128)S(1)}, u32[]{:S(2)}, u32[]{:S(2)}) async-start(f32[32,72,128]{2,1,0:T(8,128)} %collective-permute-done), calls=%async_computation | async-start | bytes 2359296 | tf_op jit(solution)/shard_map/state_to_points/all_to_all | solution.py:290
  93.6 21.1 %collective-permute-start.1 = (f32[12,192,128]{2,1,0:T(8,128)}, f32[12,192,128]{2,1,0:T(8,128)S(1)}, u32[]{:S(2)}, u32[]{:S(2)}) collective-permute-start(f32[12,192,128]{2,1,0:T(8,128)} %coefficient_stage.1), channel_id=1, source_target_pairs={{480,0},{0,32},{32,64},{64,96},{96,128},{128,160},{160,192},{192,2... | collective-permute-start | bytes 3538952 | tf_op jit(solution)/shard_map/shift_base/ppermute | solution.py:62
  134.9 6.1 %copy-start.2 = (f32[128,128]{1,0:T(8,128)S(1)}, f32[128,128]{1,0:T(8,128)}, u32[]{:S(2)}) copy-start(f32[128,128]{1,0:T(8,128)} %constant.118.clone) | copy-start | bytes 196612
  134.9 7.1 %copy-start = (f32[768,192]{1,0:T(8,128)S(1)}, f32[768,192]{1,0:T(8,128)}, u32[]{:S(2)}) copy-start(f32[768,192]{1,0:T(8,128)} %constant.117.clone) | copy-start | bytes 1769476
  134.9 48.7 %all-to-all-start.2 = ((f32[32,72,128]{2,1,0:T(8,128)}), f32[32,72,128]{2,1,0:T(8,128)S(1)}, u32[]{:S(2)}, u32[]{:S(2)}) async-start(f32[32,72,128]{2,1,0:T(8,128)} %bitcast.30), calls=%async_computation.2 | async-start | bytes 2359296 | tf_op jit(solution)/shard_map/state_to_radii/all_to_all | solution.py:290

commit v8 on v7

--- a/solution.py
+++ b/solution.py
@@ -54,6 +54,10 @@
         return jnp.dot(a, b, preferred_element_type=jnp.float32)
 
     return dot(left_high, right_high) + (dot(left_high, right_low) + dot(left_low, right_high))
+
+
+def wide(high, low):
+    return jnp.concatenate([jnp.concatenate([high, low], 1), jnp.concatenate([high, jnp.zeros_like(low)], 1)], 0)
 
 
 def from_behind(block, axis, distance):
@@ -94,7 +98,11 @@
 def filter_pair(first, second, table_t, table_z):
     count_z = first.shape[1]
     half = first.shape[0] // 2
-    both = product(split(jnp.concatenate([first, second], 1)), table_z)
+    both = []
+    for plane in (first, second):
+        plane = jnp.dot(jnp.concatenate(split(plane), 1), table_z, preferred_element_type=jnp.float32)
+        both.append(plane[:, :count_z] + plane[:, count_z:])
+    both = jnp.concatenate(both, 1)
     even = product([table[:half] for table in table_t], split(both[:half] + both[half:]))
     odd = product([table[half:] for table in table_t], split(both[:half] - both[half:]))
     both = jnp.concatenate([even + odd, even - odd], 0)
@@ -137,10 +145,10 @@
     )(late, base)
 
 
-def first_body(field_ref, base_ref, th_ref, tl_ref, zh_ref, zl_ref, state_ref):
+def first_body(field_ref, base_ref, th_ref, tl_ref, z_ref, state_ref):
     forced = [field_ref[k] + STEP_SIZE * base_ref[k] * field_ref[k] for k in range(2)]
     table_t = (th_ref[...], tl_ref[...])
-    table_z = (zh_ref[...], zl_ref[...])
+    table_z = z_ref[...]
     pack_pair(state_ref, *filter_pair(*forced, table_t, table_z))
 
 
@@ -153,10 +161,10 @@
         first_body,
         out_shape=jax.ShapeDtypeStruct((parts, 12 * radii, count_z), jnp.float32),
         grid=(radii // 2,),
-        in_specs=[plane, plane, whole_t, whole_t, whole_z, whole_z],
+        in_specs=[plane, plane, whole_t, whole_t, whole_z],
         out_specs=pl.BlockSpec((parts, 24, count_z), lambda p: (0, p, 0)),
         name="first_stage",
-    )(field, base, *table_t, *table_z)
+    )(field, base, *table_t, table_z)
 
 
 def row_of(pair, half, point):
@@ -240,9 +248,9 @@
     )(*in_vmem(state, scale, *mix))
 
 
-def last_body(state_ref, field_ref, th_ref, tl_ref, zh_ref, zl_ref, out_ref, start, buffer, start_sems, sems):
+def last_body(state_ref, field_ref, th_ref, tl_ref, z_ref, out_ref, start, buffer, start_sems, sems):
     table_t = (th_ref[...], tl_ref[...])
-    table_z = (zh_ref[...], zl_ref[...])
+    table_z = z_ref[...]
     pairs = start.shape[0] // 2
     rows = 12 * start.shape[0]
     state_ref = state_ref.reshape(state_ref.shape[0] // rows, rows, state_ref.shape[1])
@@ -274,7 +282,7 @@
     return pl.pallas_call(
         last_body,
         out_shape=jax.ShapeDtypeStruct(field.shape, jnp.float32),
-        in_specs=[vmem, whole, vmem, vmem, vmem, vmem],
+        in_specs=[vmem, whole, vmem, vmem, vmem],
         out_specs=whole,
         scratch_shapes=[
             pltpu.VMEM(field.shape, jnp.float32),
@@ -283,7 +291,7 @@
             pltpu.SemaphoreType.DMA((field.shape[0] // 2,)),
         ],
         name="last_stage",
-    )(state, field, *in_vmem(*table_t, *table_z))
+    )(state, field, *in_vmem(*table_t, table_z))
 
 
 def swap(packed):
@@ -304,10 +312,11 @@
     with jax.named_scope("base_to_points"):
         base_points = swap(base_packed)
     with jax.named_scope("first_filter"):
-        pair_z = np.kron(np.eye(2), table_z)
+        high, low = split_constant(table_z)
+        wide_z = np.block([[high, low], [high, np.zeros_like(low)]])
         rows = np.arange(count_t // 2)
         half_t = split_constant(halves(table_t)[np.concatenate([rows, count_t + rows])])
-        filtered = first_stage(state, base[0], half_t, split_constant(pair_z), parts)
+        filtered = first_stage(state, base[0], half_t, wide_z, parts)
     with jax.named_scope("shift_state"):
         filtered = from_behind(filtered, "seg", 1)
     with jax.named_scope("shift_base"):
@@ -330,7 +339,7 @@
         index_z = jnp.where(closing, (places_z + ax_shift[0]) % count_z, places_z)
         last_t = split_array(jnp.take(jnp.asarray(halves(table_t).astype(np.float32)), index_t, axis=0))
         last_z = jnp.take(jnp.asarray(table_z.astype(np.float32)), index_z, axis=0).T
-        last_z = split_array(jnp.kron(jnp.eye(2, dtype=jnp.float32), last_z))
+        last_z = wide(*split_array(last_z))
     with jax.named_scope("last_filter"):
         return last_stage(carried.reshape(-1, count_z), state, last_t, last_z)[None]
 

time: 188 us -> 188 us (level)
  transfers between devices with their start and end apart: 5 -> 5, of which waited for: 5 -> 5; matrix products, arithmetic and copies ran while one was open for 2% -> 1% of each run, Pallas kernels for 5% -> 4%
where the time goes in v8:
time: 188 us; the launch traced here: 187 us
  waiting for transfers between devices  104 us (55%)
  Pallas kernels  40.4 us (21%)
  starting transfers between devices  38 us (20%)
  local copies, waits for them, and re-layouts  2.42 us (1%)
  between operations  2.1 us (1%)
    all_to_all x3, waiting for transfers between devices, swap(): return lax.all_to_all(packed, 'space', 0, 0, tiled=True)  72.1 us
    ppermute x2, waiting for transfers between devices, from_behind(): return lax.ppermute(block, axis, route)  31.6 us
    all_to_all x3, starting transfers between devices, swap(): return lax.all_to_all(packed, 'space', 0, 0, tiled=True)  27.2 us
    pallas_call x1, Pallas kernels, pack_stage(): pl.pallas_call(pack_body, out_shape=jax.ShapeDtypeStruct(shape, jnp.float...  26.3 us
    ppermute x2, starting transfers between devices, from_behind(): return lax.ppermute(block, axis, route)  10.8 us
    pallas_call x1, Pallas kernels, first_stage(): pl.pallas_call(first_body, out_shape=jax.ShapeDtypeStruct((parts, 12 * ra...  4.45 us
  transfers between devices with their start and end apart: 5, of which 5 were waited for; matrix products, arithmetic and copies ran while one was open for 1% of the time, Pallas kernels for 4%

profile of v8, /device:TPU:1, one launch (start us, length us, event | category | flops | bytes accessed | tf_op | source)
XLA Modules:
  0.0 186.9 jit_solution(14487290760910992729)
XLA Ops:
  0.0 26.3 %pack_stage.1 = f32[32,72,128]{2,1,0:T(8,128)} custom-call(s32[1]{0:T(128)} %bitcast.3.late_ref, f32[6,384,128]{2,1,0:T(8,128)} %bitcast.28), custom_call_target="tpu_custom_call" | custom-call | tf_op jit(solution)/shard_map/pack_base/pack_stage/pallas_call | solution.py:133
  26.3 17.0 %all-to-all-start.1 = ((f32[32,72,128]{2,1,0:T(8,128)}), f32[32,72,128]{2,1,0:T(8,128)S(1)}, u32[]{:S(2)}, u32[]{:S(2)}) async-start(f32[32,72,128]{2,1,0:T(8,128)} %pack_stage.1), calls=%async_computation.1 | async-start | bytes 2359296 | tf_op jit(solution)/shard_map/base_to_points/all_to_all | solution.py:298
  43.3 4.4 %first_stage.1 = f32[32,72,128]{2,1,0:T(8,128)} custom-call(f32[6,384,128]{2,1,0:T(8,128)} %bitcast.30, f32[6,384,128]{2,1,0:T(8,128)} %bitcast.29, bf16[384,192]{1,0:T(8,128)(2,1)} %constant.112.clone.th_ref, bf16[384,192]{1,0:T(8,128)(2,1)} %constant.113.clone.tl_ref, bf16[256,256]{1,0:T(8,128)(2,1)} %constant.114.clone.z_ref), custom_call_target="tpu_custom_call" | custom-call | tf_op jit(solution)/shard_map/first_filter/first_stage/pallas_call | solution.py:160
  47.7 5.2 %collective-permute-start = (f32[32,72,128]{2,1,0:T(8,128)}, f32[32,72,128]{2,1,0:T(8,128)}, u32[]{:S(2)}, u32[]{:S(2)}) collective-permute-start(f32[32,72,128]{2,1,0:T(8,128)} %first_stage.1), channel_id=1, source_target_pairs={{480,0},{0,32},{32,64},{64,96},{96,128},{128,160},{160,192},{192,2... | collective-permute-start | bytes 3538952 | tf_op jit(solution)/shard_map/shift_state/ppermute | solution.py:66
  52.9 17.0 %collective-permute-done = f32[32,72,128]{2,1,0:T(8,128)} collective-permute-done((f32[32,72,128]{2,1,0:T(8,128)}, f32[32,72,128]{2,1,0:T(8,128)}, u32[]{:S(2)}, u32[]{:S(2)}) %collective-permute-start) | collective-permute-done | bytes 1179680 | tf_op jit(solution)/shard_map/shift_state/ppermute | solution.py:66
  70.0 14.9 %all-to-all-done.1 = f32[32,72,128]{2,1,0:T(8,128)S(1)} async-done(((f32[32,72,128]{2,1,0:T(8,128)}), f32[32,72,128]{2,1,0:T(8,128)S(1)}, u32[]{:S(2)}, u32[]{:S(2)}) %all-to-all-start.1) | async-done | bytes 1179680 | tf_op jit(solution)/shard_map/base_to_points/all_to_all | solution.py:298
  84.9 0.0 copy-start.1
  84.9 6.2 %all-to-all-start = ((f32[32,72,128]{2,1,0:T(8,128)}), f32[32,72,128]{2,1,0:T(8,128)S(1)}, u32[]{:S(2)}, u32[]{:S(2)}) async-start(f32[32,72,128]{2,1,0:T(8,128)} %collective-permute-done), calls=%async_computation | async-start | bytes 2359296 | tf_op jit(solution)/shard_map/state_to_points/all_to_all | solution.py:298
  91.0 0.0 copy-done.1
  91.0 2.5 %coefficient_stage.1 = f32[12,192,128]{2,1,0:T(8,128)} custom-call(f32[2304,128]{1,0:T(8,128)} %bitcast.27), custom_call_target="tpu_custom_call" | custom-call | tf_op jit(solution)/shard_map/shift_base/coefficient_stage/pallas_call | solution.py:189
  93.6 5.6 %collective-permute-start.1 = (f32[12,192,128]{2,1,0:T(8,128)}, f32[12,192,128]{2,1,0:T(8,128)S(1)}, u32[]{:S(2)}, u32[]{:S(2)}) collective-permute-start(f32[12,192,128]{2,1,0:T(8,128)} %coefficient_stage.1), channel_id=1, source_target_pairs={{480,0},{0,32},{32,64},{64,96},{96,128},{128,160},{160,192},{192,2... | collective-permute-start | bytes 3538952 | tf_op jit(solution)/shard_map/shift_base/ppermute | solution.py:66
  99.2 1.3 mix_stage.1
  100.5 14.5 %collective-permute-done.1.scale_ref = f32[12,192,128]{2,1,0:T(8,128)S(1)} collective-permute-done((f32[12,192,128]{2,1,0:T(8,128)}, f32[12,192,128]{2,1,0:T(8,128)S(1)}, u32[]{:S(2)}, u32[]{:S(2)}) %collective-permute-start.1) | collective-permute-done | bytes 1179680 | tf_op jit(solution)/shard_map/shift_base/ppermute | solution.py:66
  115.1 17.4 %all-to-all-done = f32[32,72,128]{2,1,0:T(8,128)S(1)} async-done(((f32[32,72,128]{2,1,0:T(8,128)}), f32[32,72,128]{2,1,0:T(8,128)S(1)}, u32[]{:S(2)}, u32[]{:S(2)}) %all-to-all-start) | async-done | bytes 1179680 | tf_op jit(solution)/shard_map/state_to_points/all_to_all | solution.py:298
  132.5 2.4 %radial_stage.1 = f32[2304,128]{1,0:T(8,128)} custom-call(f32[2304,128]{1,0:T(8,128)S(1)} %bitcast.24, f32[12,192,128]{2,1,0:T(8,128)S(1)} %collective-permute-done.1.scale_ref, bf16[192,192]{1,0:T(8,128)(2,1)S(1)} %get-tuple-element.7.high_ref, bf16[192,192]{1,0:T(8,128)(2,1)S(1)} %get-tuple-element.8.low_ref), custom_call_target="tpu_custom_call" | custom-call | tf_op jit(solution)/shard_map/radial/radial_stage/pallas_call | solution.py:242
  134.9 0.0 copy-start.2
  134.9 0.0 copy-start
  134.9 4.1 %all-to-all-start.2 = ((f32[32,72,128]{2,1,0:T(8,128)}), f32[32,72,128]{2,1,0:T(8,128)S(1)}, u32[]{:S(2)}, u32[]{:S(2)}) async-start(f32[32,72,128]{2,1,0:T(8,128)} %bitcast.26), calls=%async_computation.2 | async-start | bytes 2359296 | tf_op jit(solution)/shard_map/state_to_radii/all_to_all | solution.py:298
  140.9 0.0 copy-done.2
  140.9 0.6 gather_fusion.1
  141.6 0.1 copy.14
  141.7 0.1 fusion.4
  141.8 0.0 copy-done
  141.8 1.7 gather_fusion
  143.5 0.1 compare_and_fusion.1
  143.6 0.1 fusion
  143.8 39.8 %all-to-all-done.2 = f32[32,72,128]{2,1,0:T(8,128)S(1)} async-done(((f32[32,72,128]{2,1,0:T(8,128)}), f32[32,72,128]{2,1,0:T(8,128)S(1)}, u32[]{:S(2)}, u32[]{:S(2)}) %all-to-all-start.2) | async-done | bytes 1179680 | tf_op jit(solution)/shard_map/state_to_radii/all_to_all | solution.py:298
  183.6 3.3 %last_stage.1 = f32[6,384,128]{2,1,0:T(8,128)} custom-call(f32[2304,128]{1,0:T(8,128)S(1)} %bitcast.25, f32[6,384,128]{2,1,0:T(8,128)} %bitcast.31, bf16[384,192]{1,0:T(8,128)(2,1)S(1)} %get-tuple-element.12.th_ref, bf16[384,192]{1,0:T(8,128)(2,1)S(1)} %get-tuple-element.11.tl_ref, bf16[256,256]{1,0:T(8,128)(2,1)S(1)} %fusion.2.z_ref), custom_call_target="tpu_custom_call" | custom-call | tf_op jit(solution)/shard_map/last_filter/last_stage/pallas_call | solution.py:282
  (8 shorter events, 0.1 us)
Async XLA Ops:
  26.3 58.5 %all-to-all-start.1 = ((f32[32,72,128]{2,1,0:T(8,128)}), f32[32,72,128]{2,1,0:T(8,128)S(1)}, u32[]{:S(2)}, u32[]{:S(2)}) async-start(f32[32,72,128]{2,1,0:T(8,128)} %pack_stage.1), calls=%async_computation.1 | async-start | bytes 2359296 | tf_op jit(solution)/shard_map/base_to_points/all_to_all | solution.py:298
  47.7 22.2 %collective-permute-start = (f32[32,72,128]{2,1,0:T(8,128)}, f32[32,72,128]{2,1,0:T(8,128)}, u32[]{:S(2)}, u32[]{:S(2)}) collective-permute-start(f32[32,72,128]{2,1,0:T(8,128)} %first_stage.1), channel_id=1, source_target_pairs={{480,0},{0,32},{32,64},{64,96},{96,128},{128,160},{160,192},{192,2... | collective-permute-start | bytes 3538952 | tf_op jit(solution)/shard_map/shift_state/ppermute | solution.py:66
  84.9 6.2 %copy-start.1 = (f32[32,72,128]{2,1,0:T(8,128)}, f32[32,72,128]{2,1,0:T(8,128)S(1)}, u32[]{:S(2)}) copy-start(f32[32,72,128]{2,1,0:T(8,128)S(1)} %all-to-all-done.1) | copy-start | bytes 3538948
  84.9 47.6 %all-to-all-start = ((f32[32,72,128]{2,1,0:T(8,128)}), f32[32,72,128]{2,1,0:T(8,128)S(1)}, u32[]{:S(2)}, u32[]{:S(2)}) async-start(f32[32,72,128]{2,1,0:T(8,128)} %collective-permute-done), calls=%async_computation | async-start | bytes 2359296 | tf_op jit(solution)/shard_map/state_to_points/all_to_all | solution.py:298
  93.6 21.5 %collective-permute-start.1 = (f32[12,192,128]{2,1,0:T(8,128)}, f32[12,192,128]{2,1,0:T(8,128)S(1)}, u32[]{:S(2)}, u32[]{:S(2)}) collective-permute-start(f32[12,192,128]{2,1,0:T(8,128)} %coefficient_stage.1), channel_id=1, source_target_pairs={{480,0},{0,32},{32,64},{64,96},{96,128},{128,160},{160,192},{192,2... | collective-permute-start | bytes 3538952 | tf_op jit(solution)/shard_map/shift_base/ppermute | solution.py:66
  134.9 6.1 %copy-start.2 = (f32[128,128]{1,0:T(8,128)S(1)}, f32[128,128]{1,0:T(8,128)}, u32[]{:S(2)}) copy-start(f32[128,128]{1,0:T(8,128)} %constant.117.clone) | copy-start | bytes 196612
  134.9 7.0 %copy-start = (f32[768,192]{1,0:T(8,128)S(1)}, f32[768,192]{1,0:T(8,128)}, u32[]{:S(2)}) copy-start(f32[768,192]{1,0:T(8,128)} %constant.116.clone) | copy-start | bytes 1769476
  134.9 48.7 %all-to-all-start.2 = ((f32[32,72,128]{2,1,0:T(8,128)}), f32[32,72,128]{2,1,0:T(8,128)S(1)}, u32[]{:S(2)}, u32[]{:S(2)}) async-start(f32[32,72,128]{2,1,0:T(8,128)} %bitcast.26), calls=%async_computation.2 | async-start | bytes 2359296 | tf_op jit(solution)/shard_map/state_to_radii/all_to_all | solution.py:298

commit v9 on v8

--- a/solution.py
+++ b/solution.py
@@ -218,11 +218,22 @@
     )(mix, order)
 
 
-def radial_body(state_ref, scale_ref, high_ref, low_ref, out_ref):
+def radial_body(state_ref, scale_ref, high_ref, low_ref, result_ref, out_ref, sems):
     parts = scale_ref.shape[1] // 6
     count_z = scale_ref.shape[2]
     stride = out_ref.shape[0] // parts
     mix = (high_ref[...], low_ref[...])
+    blocks = out_ref.reshape(parts, stride, count_z)
+    copies = []
+
+    def send(first, rows):
+        for p in range(3):
+            window = pl.ds(24 * p + first, rows)
+            copies.append(
+                pltpu.make_async_copy(blocks.at[:, window, :], result_ref.at[:, window, :], sems.at[len(copies)])
+            )
+            copies[-1].start()
+
     for point in range(0, scale_ref.shape[0], 2):
         state = jnp.concatenate([load_points(state_ref, point + k, parts) for k in range(2)], 1)
         scale = jnp.concatenate([scale_ref[point + k] for k in range(2)], 1)
@@ -235,15 +246,21 @@
                     out_ref[pl.ds(row_of(p, e, point + k), parts, stride), :] = state[
                         radius : radius + parts, k * count_z : (k + 1) * count_z
                     ]
-
-
-def radial_stage(state, scale, mix):
+        if point + 2 == TILE:
+            send(0, 2 * TILE)
+    send(2 * TILE, TILE)
+    for copy in copies:
+        copy.wait()
+
+
+def radial_stage(state, scale, mix, parts):
     vmem = pl.BlockSpec(memory_space=pltpu.VMEM)
     return pl.pallas_call(
         radial_body,
-        out_shape=jax.ShapeDtypeStruct(state.shape, jnp.float32),
+        out_shape=jax.ShapeDtypeStruct((parts, state.shape[0] // parts, state.shape[1]), jnp.float32),
         in_specs=[vmem] * 4,
-        out_specs=vmem,
+        out_specs=pl.BlockSpec(memory_space=pltpu.HBM),
+        scratch_shapes=[pltpu.VMEM(state.shape, jnp.float32), pltpu.SemaphoreType.DMA((6,))],
         name="radial_stage",
     )(*in_vmem(state, scale, *mix))
 
@@ -325,9 +342,9 @@
     with jax.named_scope("state_to_points"):
         points = swap(filtered)
     with jax.named_scope("radial"):
-        points = radial_stage(points.reshape(-1, count_z), scale, mix_stage(radial_step, parts))
+        points = radial_stage(points.reshape(-1, count_z), scale, mix_stage(radial_step, parts), parts)
     with jax.named_scope("state_to_radii"):
-        carried = swap(points.reshape(parts, -1, count_z))
+        carried = swap(points)
 
     with jax.named_scope("closing_tables"):
         closing = segment == first_segment[0] % lax.axis_size("seg")

time: 188 us -> 187 us (level)
  transfers between devices with their start and end apart: 5 -> 5, of which waited for: 5 -> 5; matrix products, arithmetic and copies ran while one was open for 1% -> 2% of each run, Pallas kernels for 4% -> 4%
where the time goes in v9:
time: 187 us
  waiting for transfers between devices  104 us (56%)
  Pallas kernels  40.2 us (21%)
  starting transfers between devices  38 us (20%)
  local copies, waits for them, and re-layouts  2.42 us (1%)
  between operations  2.12 us (1%)
    all_to_all x3, waiting for transfers between devices, swap(): return lax.all_to_all(packed, 'space', 0, 0, tiled=True)  72 us
    ppermute x2, waiting for transfers between devices, from_behind(): return lax.ppermute(block, axis, route)  31.6 us
    all_to_all x3, starting transfers between devices, swap(): return lax.all_to_all(packed, 'space', 0, 0, tiled=True)  27.2 us
    pallas_call x1, Pallas kernels, pack_stage(): pl.pallas_call(pack_body, out_shape=jax.ShapeDtypeStruct(shape, jnp.float...  26.3 us
    ppermute x2, starting transfers between devices, from_behind(): return lax.ppermute(block, axis, route)  10.8 us
    pallas_call x1, Pallas kernels, first_stage(): pl.pallas_call(first_body, out_shape=jax.ShapeDtypeStruct((parts, 12 * ra...  4.45 us
  transfers between devices with their start and end apart: 5, of which 5 were waited for; matrix products, arithmetic and copies ran while one was open for 2% of the time, Pallas kernels for 4%

profile of v9, /device:TPU:1, one launch (start us, length us, event | category | flops | bytes accessed | tf_op | source)
XLA Modules:
  0.0 186.7 jit_solution(14117624390669504428)
XLA Ops:
  0.0 26.3 %pack_stage.1 = f32[32,72,128]{2,1,0:T(8,128)} custom-call(s32[1]{0:T(128)} %bitcast.3.late_ref, f32[6,384,128]{2,1,0:T(8,128)} %bitcast.26), custom_call_target="tpu_custom_call" | custom-call | tf_op jit(solution)/shard_map/pack_base/pack_stage/pallas_call | solution.py:133
  26.3 17.0 %all-to-all-start.1 = ((f32[32,72,128]{2,1,0:T(8,128)}), f32[32,72,128]{2,1,0:T(8,128)S(1)}, u32[]{:S(2)}, u32[]{:S(2)}) async-start(f32[32,72,128]{2,1,0:T(8,128)} %pack_stage.1), calls=%async_computation.1 | async-start | bytes 2359296 | tf_op jit(solution)/shard_map/base_to_points/all_to_all | solution.py:315
  43.3 4.4 %first_stage.1 = f32[32,72,128]{2,1,0:T(8,128)} custom-call(f32[6,384,128]{2,1,0:T(8,128)} %bitcast.28, f32[6,384,128]{2,1,0:T(8,128)} %bitcast.27, bf16[384,192]{1,0:T(8,128)(2,1)} %constant.112.clone.th_ref, bf16[384,192]{1,0:T(8,128)(2,1)} %constant.113.clone.tl_ref, bf16[256,256]{1,0:T(8,128)(2,1)} %constant.114.clone.z_ref), custom_call_target="tpu_custom_call" | custom-call | tf_op jit(solution)/shard_map/first_filter/first_stage/pallas_call | solution.py:160
  47.7 5.2 %collective-permute-start = (f32[32,72,128]{2,1,0:T(8,128)}, f32[32,72,128]{2,1,0:T(8,128)}, u32[]{:S(2)}, u32[]{:S(2)}) collective-permute-start(f32[32,72,128]{2,1,0:T(8,128)} %first_stage.1), channel_id=1, source_target_pairs={{480,0},{0,32},{32,64},{64,96},{96,128},{128,160},{160,192},{192,2... | collective-permute-start | bytes 3538952 | tf_op jit(solution)/shard_map/shift_state/ppermute | solution.py:66
  52.9 17.0 %collective-permute-done = f32[32,72,128]{2,1,0:T(8,128)} collective-permute-done((f32[32,72,128]{2,1,0:T(8,128)}, f32[32,72,128]{2,1,0:T(8,128)}, u32[]{:S(2)}, u32[]{:S(2)}) %collective-permute-start) | collective-permute-done | bytes 1179680 | tf_op jit(solution)/shard_map/shift_state/ppermute | solution.py:66
  70.0 14.9 %all-to-all-done.1 = f32[32,72,128]{2,1,0:T(8,128)S(1)} async-done(((f32[32,72,128]{2,1,0:T(8,128)}), f32[32,72,128]{2,1,0:T(8,128)S(1)}, u32[]{:S(2)}, u32[]{:S(2)}) %all-to-all-start.1) | async-done | bytes 1179680 | tf_op jit(solution)/shard_map/base_to_points/all_to_all | solution.py:315
  84.9 0.0 copy-start.1
  84.9 6.2 %all-to-all-start = ((f32[32,72,128]{2,1,0:T(8,128)}), f32[32,72,128]{2,1,0:T(8,128)S(1)}, u32[]{:S(2)}, u32[]{:S(2)}) async-start(f32[32,72,128]{2,1,0:T(8,128)} %collective-permute-done), calls=%async_computation | async-start | bytes 2359296 | tf_op jit(solution)/shard_map/state_to_points/all_to_all | solution.py:315
  91.0 0.0 copy-done.1
  91.0 2.5 %coefficient_stage.1 = f32[12,192,128]{2,1,0:T(8,128)} custom-call(f32[2304,128]{1,0:T(8,128)} %bitcast.25), custom_call_target="tpu_custom_call" | custom-call | tf_op jit(solution)/shard_map/shift_base/coefficient_stage/pallas_call | solution.py:189
  93.6 5.6 %collective-permute-start.1 = (f32[12,192,128]{2,1,0:T(8,128)}, f32[12,192,128]{2,1,0:T(8,128)S(1)}, u32[]{:S(2)}, u32[]{:S(2)}) collective-permute-start(f32[12,192,128]{2,1,0:T(8,128)} %coefficient_stage.1), channel_id=1, source_target_pairs={{480,0},{0,32},{32,64},{64,96},{96,128},{128,160},{160,192},{192,2... | collective-permute-start | bytes 3538952 | tf_op jit(solution)/shard_map/shift_base/ppermute | solution.py:66
  99.2 1.3 mix_stage.1
  100.5 14.5 %collective-permute-done.1.scale_ref = f32[12,192,128]{2,1,0:T(8,128)S(1)} collective-permute-done((f32[12,192,128]{2,1,0:T(8,128)}, f32[12,192,128]{2,1,0:T(8,128)S(1)}, u32[]{:S(2)}, u32[]{:S(2)}) %collective-permute-start.1) | collective-permute-done | bytes 1179680 | tf_op jit(solution)/shard_map/shift_base/ppermute | solution.py:66
  115.1 17.4 %all-to-all-done = f32[32,72,128]{2,1,0:T(8,128)S(1)} async-done(((f32[32,72,128]{2,1,0:T(8,128)}), f32[32,72,128]{2,1,0:T(8,128)S(1)}, u32[]{:S(2)}, u32[]{:S(2)}) %all-to-all-start) | async-done | bytes 1179680 | tf_op jit(solution)/shard_map/state_to_points/all_to_all | solution.py:315
  132.5 2.2 %radial_stage.1 = f32[32,72,128]{2,1,0:T(8,128)} custom-call(f32[2304,128]{1,0:T(8,128)S(1)} %bitcast.23, f32[12,192,128]{2,1,0:T(8,128)S(1)} %collective-permute-done.1.scale_ref, bf16[192,192]{1,0:T(8,128)(2,1)S(1)} %get-tuple-element.7.high_ref, bf16[192,192]{1,0:T(8,128)(2,1)S(1)} %get-tuple-element.8.low_ref), custom_call_target="tpu_custom_call" | custom-call | tf_op jit(solution)/shard_map/radial/radial_stage/pallas_call | solution.py:258
  134.7 0.0 copy-start.2
  134.7 0.0 copy-start
  134.7 4.1 %all-to-all-start.2 = ((f32[32,72,128]{2,1,0:T(8,128)}), f32[32,72,128]{2,1,0:T(8,128)S(1)}, u32[]{:S(2)}, u32[]{:S(2)}) async-start(f32[32,72,128]{2,1,0:T(8,128)} %radial_stage.1), calls=%async_computation.2 | async-start | bytes 2359296 | tf_op jit(solution)/shard_map/state_to_radii/all_to_all | solution.py:315
  140.8 0.0 copy-done.2
  140.8 0.6 gather_fusion.1
  141.5 0.1 copy.14
  141.6 0.1 fusion.4
  141.7 0.0 copy-done
  141.7 1.7 gather_fusion
  143.4 0.1 compare_and_fusion.1
  143.5 0.1 fusion
  143.6 39.7 %all-to-all-done.2 = f32[32,72,128]{2,1,0:T(8,128)S(1)} async-done(((f32[32,72,128]{2,1,0:T(8,128)}), f32[32,72,128]{2,1,0:T(8,128)S(1)}, u32[]{:S(2)}, u32[]{:S(2)}) %all-to-all-start.2) | async-done | bytes 1179680 | tf_op jit(solution)/shard_map/state_to_radii/all_to_all | solution.py:315
  183.4 3.4 %last_stage.1 = f32[6,384,128]{2,1,0:T(8,128)} custom-call(f32[2304,128]{1,0:T(8,128)S(1)} %bitcast.24, f32[6,384,128]{2,1,0:T(8,128)} %bitcast.29, bf16[384,192]{1,0:T(8,128)(2,1)S(1)} %get-tuple-element.12.th_ref, bf16[384,192]{1,0:T(8,128)(2,1)S(1)} %get-tuple-element.11.tl_ref, bf16[256,256]{1,0:T(8,128)(2,1)S(1)} %fusion.2.z_ref), custom_call_target="tpu_custom_call" | custom-call | tf_op jit(solution)/shard_map/last_filter/last_stage/pallas_call | solution.py:299
  (8 shorter events, 0.1 us)
Async XLA Ops:
  26.3 58.5 %all-to-all-start.1 = ((f32[32,72,128]{2,1,0:T(8,128)}), f32[32,72,128]{2,1,0:T(8,128)S(1)}, u32[]{:S(2)}, u32[]{:S(2)}) async-start(f32[32,72,128]{2,1,0:T(8,128)} %pack_stage.1), calls=%async_computation.1 | async-start | bytes 2359296 | tf_op jit(solution)/shard_map/base_to_points/all_to_all | solution.py:315
  47.7 22.2 %collective-permute-start = (f32[32,72,128]{2,1,0:T(8,128)}, f32[32,72,128]{2,1,0:T(8,128)}, u32[]{:S(2)}, u32[]{:S(2)}) collective-permute-start(f32[32,72,128]{2,1,0:T(8,128)} %first_stage.1), channel_id=1, source_target_pairs={{480,0},{0,32},{32,64},{64,96},{96,128},{128,160},{160,192},{192,2... | collective-permute-start | bytes 3538952 | tf_op jit(solution)/shard_map/shift_state/ppermute | solution.py:66
  84.9 6.2 %copy-start.1 = (f32[32,72,128]{2,1,0:T(8,128)}, f32[32,72,128]{2,1,0:T(8,128)S(1)}, u32[]{:S(2)}) copy-start(f32[32,72,128]{2,1,0:T(8,128)S(1)} %all-to-all-done.1) | copy-start | bytes 3538948
  84.9 47.6 %all-to-all-start = ((f32[32,72,128]{2,1,0:T(8,128)}), f32[32,72,128]{2,1,0:T(8,128)S(1)}, u32[]{:S(2)}, u32[]{:S(2)}) async-start(f32[32,72,128]{2,1,0:T(8,128)} %collective-permute-done), calls=%async_computation | async-start | bytes 2359296 | tf_op jit(solution)/shard_map/state_to_points/all_to_all | solution.py:315
  93.6 21.5 %collective-permute-start.1 = (f32[12,192,128]{2,1,0:T(8,128)}, f32[12,192,128]{2,1,0:T(8,128)S(1)}, u32[]{:S(2)}, u32[]{:S(2)}) collective-permute-start(f32[12,192,128]{2,1,0:T(8,128)} %coefficient_stage.1), channel_id=1, source_target_pairs={{480,0},{0,32},{32,64},{64,96},{96,128},{128,160},{160,192},{192,2... | collective-permute-start | bytes 3538952 | tf_op jit(solution)/shard_map/shift_base/ppermute | solution.py:66
  134.7 6.1 %copy-start.2 = (f32[128,128]{1,0:T(8,128)S(1)}, f32[128,128]{1,0:T(8,128)}, u32[]{:S(2)}) copy-start(f32[128,128]{1,0:T(8,128)} %constant.117.clone) | copy-start | bytes 196612
  134.7 7.0 %copy-start = (f32[768,192]{1,0:T(8,128)S(1)}, f32[768,192]{1,0:T(8,128)}, u32[]{:S(2)}) copy-start(f32[768,192]{1,0:T(8,128)} %constant.116.clone) | copy-start | bytes 1769476
  134.7 48.6 %all-to-all-start.2 = ((f32[32,72,128]{2,1,0:T(8,128)}), f32[32,72,128]{2,1,0:T(8,128)S(1)}, u32[]{:S(2)}, u32[]{:S(2)}) async-start(f32[32,72,128]{2,1,0:T(8,128)} %radial_stage.1), calls=%async_computation.2 | async-start | bytes 2359296 | tf_op jit(solution)/shard_map/state_to_radii/all_to_all | solution.py:315

commit v10 on v8

--- a/solution.py
+++ b/solution.py
@@ -11,7 +11,7 @@
 
 STEP_SIZE = 0.25
 VISCOUS_RATE = 1.5e-05
-STAGGER = 25000
+STAGGER = 24000
 TILE = 8
 
 

time: 188 us -> 189 us (level)
  waiting for transfers between devices: 104 us -> 106 us
    all_to_all x3, waiting for transfers between devices: 72.1 us -> 74.2 us  [swap(): return lax.all_to_all(packed, 'space', 0, 0, tiled=True)]
where the time goes in v10:
time: 189 us; the launch traced here: 188 us
  waiting for transfers between devices  106 us (56%)
  Pallas kernels  39.4 us (21%)
  starting transfers between devices  38.2 us (20%)
  local copies, waits for them, and re-layouts  2.42 us (1%)
  between operations  2.1 us (1%)
    all_to_all x3, waiting for transfers between devices, swap(): return lax.all_to_all(packed, 'space', 0, 0, tiled=True)  74.2 us
    ppermute x2, waiting for transfers between devices, from_behind(): return lax.ppermute(block, axis, route)  31.3 us
    all_to_all x3, starting transfers between devices, swap(): return lax.all_to_all(packed, 'space', 0, 0, tiled=True)  27.1 us
    pallas_call x1, Pallas kernels, pack_stage(): pl.pallas_call(pack_body, out_shape=jax.ShapeDtypeStruct(shape, jnp.float...  25.3 us
    ppermute x2, starting transfers between devices, from_behind(): return lax.ppermute(block, axis, route)  11.1 us
    pallas_call x1, Pallas kernels, first_stage(): pl.pallas_call(first_body, out_shape=jax.ShapeDtypeStruct((parts, 12 * ra...  4.45 us
  transfers between devices with their start and end apart: 5, of which 5 were waited for; matrix products, arithmetic and copies ran while one was open for 1% of the time, Pallas kernels for 4%

profile of v10, /device:TPU:1, one launch (start us, length us, event | category | flops | bytes accessed | tf_op | source)
XLA Modules:
  0.0 188.1 jit_solution(4309094913939863418)
XLA Ops:
  0.0 25.3 %pack_stage.1 = f32[32,72,128]{2,1,0:T(8,128)} custom-call(s32[1]{0:T(128)} %bitcast.3.late_ref, f32[6,384,128]{2,1,0:T(8,128)} %bitcast.28), custom_call_target="tpu_custom_call" | custom-call | tf_op jit(solution)/shard_map/pack_base/pack_stage/pallas_call | solution.py:133
  25.3 17.0 %all-to-all-start.1 = ((f32[32,72,128]{2,1,0:T(8,128)}), f32[32,72,128]{2,1,0:T(8,128)S(1)}, u32[]{:S(2)}, u32[]{:S(2)}) async-start(f32[32,72,128]{2,1,0:T(8,128)} %pack_stage.1), calls=%async_computation.1 | async-start | bytes 2359296 | tf_op jit(solution)/shard_map/base_to_points/all_to_all | solution.py:298
  42.3 4.4 %first_stage.1 = f32[32,72,128]{2,1,0:T(8,128)} custom-call(f32[6,384,128]{2,1,0:T(8,128)} %bitcast.30, f32[6,384,128]{2,1,0:T(8,128)} %bitcast.29, bf16[384,192]{1,0:T(8,128)(2,1)} %constant.112.clone.th_ref, bf16[384,192]{1,0:T(8,128)(2,1)} %constant.113.clone.tl_ref, bf16[256,256]{1,0:T(8,128)(2,1)} %constant.114.clone.z_ref), custom_call_target="tpu_custom_call" | custom-call | tf_op jit(solution)/shard_map/first_filter/first_stage/pallas_call | solution.py:160
  46.7 5.2 %collective-permute-start = (f32[32,72,128]{2,1,0:T(8,128)}, f32[32,72,128]{2,1,0:T(8,128)}, u32[]{:S(2)}, u32[]{:S(2)}) collective-permute-start(f32[32,72,128]{2,1,0:T(8,128)} %first_stage.1), channel_id=1, source_target_pairs={{480,0},{0,32},{32,64},{64,96},{96,128},{128,160},{160,192},{192,2... | collective-permute-start | bytes 3538952 | tf_op jit(solution)/shard_map/shift_state/ppermute | solution.py:66
  51.9 16.5 %collective-permute-done = f32[32,72,128]{2,1,0:T(8,128)} collective-permute-done((f32[32,72,128]{2,1,0:T(8,128)}, f32[32,72,128]{2,1,0:T(8,128)}, u32[]{:S(2)}, u32[]{:S(2)}) %collective-permute-start) | collective-permute-done | bytes 1179680 | tf_op jit(solution)/shard_map/shift_state/ppermute | solution.py:66
  68.5 16.3 %all-to-all-done.1 = f32[32,72,128]{2,1,0:T(8,128)S(1)} async-done(((f32[32,72,128]{2,1,0:T(8,128)}), f32[32,72,128]{2,1,0:T(8,128)S(1)}, u32[]{:S(2)}, u32[]{:S(2)}) %all-to-all-start.1) | async-done | bytes 1179680 | tf_op jit(solution)/shard_map/base_to_points/all_to_all | solution.py:298
  84.7 0.0 copy-start.1
  84.7 6.1 %all-to-all-start = ((f32[32,72,128]{2,1,0:T(8,128)}), f32[32,72,128]{2,1,0:T(8,128)S(1)}, u32[]{:S(2)}, u32[]{:S(2)}) async-start(f32[32,72,128]{2,1,0:T(8,128)} %collective-permute-done), calls=%async_computation | async-start | bytes 2359296 | tf_op jit(solution)/shard_map/state_to_points/all_to_all | solution.py:298
  90.8 0.0 copy-done.1
  90.8 2.5 %coefficient_stage.1 = f32[12,192,128]{2,1,0:T(8,128)} custom-call(f32[2304,128]{1,0:T(8,128)} %bitcast.27), custom_call_target="tpu_custom_call" | custom-call | tf_op jit(solution)/shard_map/shift_base/coefficient_stage/pallas_call | solution.py:189
  93.3 5.9 %collective-permute-start.1 = (f32[12,192,128]{2,1,0:T(8,128)}, f32[12,192,128]{2,1,0:T(8,128)S(1)}, u32[]{:S(2)}, u32[]{:S(2)}) collective-permute-start(f32[12,192,128]{2,1,0:T(8,128)} %coefficient_stage.1), channel_id=1, source_target_pairs={{480,0},{0,32},{32,64},{64,96},{96,128},{128,160},{160,192},{192,2... | collective-permute-start | bytes 3538952 | tf_op jit(solution)/shard_map/shift_base/ppermute | solution.py:66
  99.3 1.3 mix_stage.1
  100.6 14.8 %collective-permute-done.1.scale_ref = f32[12,192,128]{2,1,0:T(8,128)S(1)} collective-permute-done((f32[12,192,128]{2,1,0:T(8,128)}, f32[12,192,128]{2,1,0:T(8,128)S(1)}, u32[]{:S(2)}, u32[]{:S(2)}) %collective-permute-start.1) | collective-permute-done | bytes 1179680 | tf_op jit(solution)/shard_map/shift_base/ppermute | solution.py:66
  115.4 16.9 %all-to-all-done = f32[32,72,128]{2,1,0:T(8,128)S(1)} async-done(((f32[32,72,128]{2,1,0:T(8,128)}), f32[32,72,128]{2,1,0:T(8,128)S(1)}, u32[]{:S(2)}, u32[]{:S(2)}) %all-to-all-start) | async-done | bytes 1179680 | tf_op jit(solution)/shard_map/state_to_points/all_to_all | solution.py:298
  132.4 2.4 %radial_stage.1 = f32[2304,128]{1,0:T(8,128)} custom-call(f32[2304,128]{1,0:T(8,128)S(1)} %bitcast.24, f32[12,192,128]{2,1,0:T(8,128)S(1)} %collective-permute-done.1.scale_ref, bf16[192,192]{1,0:T(8,128)(2,1)S(1)} %get-tuple-element.7.high_ref, bf16[192,192]{1,0:T(8,128)(2,1)S(1)} %get-tuple-element.8.low_ref), custom_call_target="tpu_custom_call" | custom-call | tf_op jit(solution)/shard_map/radial/radial_stage/pallas_call | solution.py:242
  134.8 0.0 copy-start.2
  134.8 0.0 copy-start
  134.8 4.1 %all-to-all-start.2 = ((f32[32,72,128]{2,1,0:T(8,128)}), f32[32,72,128]{2,1,0:T(8,128)S(1)}, u32[]{:S(2)}, u32[]{:S(2)}) async-start(f32[32,72,128]{2,1,0:T(8,128)} %bitcast.26), calls=%async_computation.2 | async-start | bytes 2359296 | tf_op jit(solution)/shard_map/state_to_radii/all_to_all | solution.py:298
  140.8 0.0 copy-done.2
  140.8 0.7 gather_fusion.1
  141.5 0.1 copy.14
  141.6 0.1 fusion.4
  141.7 0.0 copy-done
  141.7 1.7 gather_fusion
  143.4 0.1 compare_and_fusion.1
  143.5 0.1 fusion
  143.7 41.0 %all-to-all-done.2 = f32[32,72,128]{2,1,0:T(8,128)S(1)} async-done(((f32[32,72,128]{2,1,0:T(8,128)}), f32[32,72,128]{2,1,0:T(8,128)S(1)}, u32[]{:S(2)}, u32[]{:S(2)}) %all-to-all-start.2) | async-done | bytes 1179680 | tf_op jit(solution)/shard_map/state_to_radii/all_to_all | solution.py:298
  184.7 3.3 %last_stage.1 = f32[6,384,128]{2,1,0:T(8,128)} custom-call(f32[2304,128]{1,0:T(8,128)S(1)} %bitcast.25, f32[6,384,128]{2,1,0:T(8,128)} %bitcast.31, bf16[384,192]{1,0:T(8,128)(2,1)S(1)} %get-tuple-element.12.th_ref, bf16[384,192]{1,0:T(8,128)(2,1)S(1)} %get-tuple-element.11.tl_ref, bf16[256,256]{1,0:T(8,128)(2,1)S(1)} %fusion.2.z_ref), custom_call_target="tpu_custom_call" | custom-call | tf_op jit(solution)/shard_map/last_filter/last_stage/pallas_call | solution.py:282
  (8 shorter events, 0.1 us)
Async XLA Ops:
  25.3 59.4 %all-to-all-start.1 = ((f32[32,72,128]{2,1,0:T(8,128)}), f32[32,72,128]{2,1,0:T(8,128)S(1)}, u32[]{:S(2)}, u32[]{:S(2)}) async-start(f32[32,72,128]{2,1,0:T(8,128)} %pack_stage.1), calls=%async_computation.1 | async-start | bytes 2359296 | tf_op jit(solution)/shard_map/base_to_points/all_to_all | solution.py:298
  46.7 21.7 %collective-permute-start = (f32[32,72,128]{2,1,0:T(8,128)}, f32[32,72,128]{2,1,0:T(8,128)}, u32[]{:S(2)}, u32[]{:S(2)}) collective-permute-start(f32[32,72,128]{2,1,0:T(8,128)} %first_stage.1), channel_id=1, source_target_pairs={{480,0},{0,32},{32,64},{64,96},{96,128},{128,160},{160,192},{192,2... | collective-permute-start | bytes 3538952 | tf_op jit(solution)/shard_map/shift_state/ppermute | solution.py:66
  84.7 6.1 %copy-start.1 = (f32[32,72,128]{2,1,0:T(8,128)}, f32[32,72,128]{2,1,0:T(8,128)S(1)}, u32[]{:S(2)}) copy-start(f32[32,72,128]{2,1,0:T(8,128)S(1)} %all-to-all-done.1) | copy-start | bytes 3538948
  84.7 47.6 %all-to-all-start = ((f32[32,72,128]{2,1,0:T(8,128)}), f32[32,72,128]{2,1,0:T(8,128)S(1)}, u32[]{:S(2)}, u32[]{:S(2)}) async-start(f32[32,72,128]{2,1,0:T(8,128)} %collective-permute-done), calls=%async_computation | async-start | bytes 2359296 | tf_op jit(solution)/shard_map/state_to_points/all_to_all | solution.py:298
  93.3 22.1 %collective-permute-start.1 = (f32[12,192,128]{2,1,0:T(8,128)}, f32[12,192,128]{2,1,0:T(8,128)S(1)}, u32[]{:S(2)}, u32[]{:S(2)}) collective-permute-start(f32[12,192,128]{2,1,0:T(8,128)} %coefficient_stage.1), channel_id=1, source_target_pairs={{480,0},{0,32},{32,64},{64,96},{96,128},{128,160},{160,192},{192,2... | collective-permute-start | bytes 3538952 | tf_op jit(solution)/shard_map/shift_base/ppermute | solution.py:66
  134.8 6.1 %copy-start.2 = (f32[128,128]{1,0:T(8,128)S(1)}, f32[128,128]{1,0:T(8,128)}, u32[]{:S(2)}) copy-start(f32[128,128]{1,0:T(8,128)} %constant.117.clone) | copy-start | bytes 196612
  134.8 7.0 %copy-start = (f32[768,192]{1,0:T(8,128)S(1)}, f32[768,192]{1,0:T(8,128)}, u32[]{:S(2)}) copy-start(f32[768,192]{1,0:T(8,128)} %constant.116.clone) | copy-start | bytes 1769476
  134.8 50.0 %all-to-all-start.2 = ((f32[32,72,128]{2,1,0:T(8,128)}), f32[32,72,128]{2,1,0:T(8,128)S(1)}, u32[]{:S(2)}, u32[]{:S(2)}) async-start(f32[32,72,128]{2,1,0:T(8,128)} %bitcast.26), calls=%async_computation.2 | async-start | bytes 2359296 | tf_op jit(solution)/shard_map/state_to_radii/all_to_all | solution.py:298
